TPU v7x, 256 devices: a whole 4x4x8 slice. The times are simulated.
256 devices in a mesh: dp: 16 (over x, y), latent: 16 (over z, core).
Axes of the slice: x: 4, y: 4, z: 8, core: 2. Of those that a mesh axis runs over, the one named last changes fastest.
Arguments:
- queries: bfloat16 [8192, 2048], P(('dp', 'latent')), may hold values from -32 to 32, as said below
- cache_keys: bfloat16 [256, 512, 1024], P(('dp', 'latent')), may hold values from -6 to 6
- cache_values: bfloat16 [256, 512, 1024], P(('dp', 'latent')), may hold values from -96 to 96
- positions: int32 [8192], P(('dp', 'latent')), may hold values from 224 to 511, as said below
- shuffle: int32 [8192], P(('dp', 'latent')), may hold values from 0 to 8191, as said below
- enc_weight: bfloat16 [2048, 16384], P(None, 'latent'), may hold values from -0.125 to 0.125
- enc_bias: float32 [16384], P('latent'), may hold values from -3 to 3
- dec_weight: bfloat16 [16384, 2048], P('latent'), may hold values from -0.046875 to 0.046875
- dec_bias: float32 [2048], replicated, may hold values from -3 to 3
Outputs:
- rebuilt: bfloat16 [8192, 2048], P(('dp', 'latent'))
- grad_enc: float32 [2048, 16384], P('dp', 'latent')
- grad_dec: float32 [16384, 2048], P('latent', 'dp')
Inputs may be any that keep to these rules, and one draw needn't show every extreme that they name: `queries`: entries are finite; a few rows may be aligned with keys of their sequence. The rows of one sequence have consecutive positions ending at its length minus one; lengths lie between 256 and 512, and sequence 0 has length 512. A permutation of 0 to 8191. Row r and its place shuffle[r] lie in sequences r // 32 and shuffle[r] // 32 that are equal modulo 512 // 32; from each such sequence exactly 2 rows go to each such sequence.
All inputs are finite; a program needn't handle non-finite values.
Results may differ from a plain program's by a relative error of at most 0.012.
Values may be sent and summed in bfloat16 or wider, within the bound.
A program may use at most 128 MiB of HBM per device.

v0:
```python
import jax
import jax.numpy as jnp
from jax import lax
from jax.sharding import PartitionSpec as P

HEAD_DIM = 256


sharpness = 4.0
sparsity_weight = 1.0
epsilon = 1e-06


def attend(queries, cache_keys, cache_values, positions):
    rows_here = queries.shape[0]
    kv_heads = cache_keys.shape[-1] // HEAD_DIM
    grouped = queries.reshape(rows_here, kv_heads, -1, HEAD_DIM)
    keys_local = cache_keys[0].reshape(-1, kv_heads, HEAD_DIM)
    values_local = cache_values[0].reshape(-1, kv_heads, HEAD_DIM)
    scores = jnp.einsum(
        "qgid,kgd->gqik", grouped, keys_local, preferred_element_type=jnp.float32
    ) * HEAD_DIM ** (-0.5)
    slot_index = jnp.arange(keys_local.shape[0])
    visible = slot_index[None, None, None, :] <= positions[None, :, None, None]
    scores = jnp.where(visible, scores, -jnp.inf)
    highest = jnp.max(scores, axis=-1, keepdims=True)
    weights = jnp.exp(scores - highest)
    attn_probs = (weights / jnp.sum(weights, axis=-1, keepdims=True)).astype(jnp.bfloat16)
    head_mix = jnp.einsum(
        "gqik,kgd->qgid", attn_probs, values_local, preferred_element_type=jnp.float32
    )
    return head_mix.reshape(rows_here, -1).astype(jnp.bfloat16)


def shuffle_rows(moving, shuffle):
    data_size = lax.axis_size("dp")
    latent_size = lax.axis_size("latent")
    rows_here = moving.shape[0]
    per_peer = rows_here // data_size
    target = shuffle // (rows_here * latent_size)
    send_order = jnp.argsort(target, stable=True)
    outgoing = moving[send_order].reshape(data_size, per_peer, moving.shape[1])
    places = (shuffle[send_order] % rows_here).reshape(data_size, per_peer)
    arrived, arrival_slots = (
        lax.all_to_all(outgoing, "dp", split_axis=0, concat_axis=0, tiled=True),
        lax.all_to_all(places, "dp", split_axis=0, concat_axis=0, tiled=True),
    )
    arrived = arrived.reshape(rows_here, moving.shape[1])
    arrival_slots = arrival_slots.reshape(rows_here)
    return arrived[jnp.argsort(arrival_slots)]


def shards(
    queries,
    cache_keys,
    cache_values,
    positions,
    shuffle,
    enc_weight,
    enc_bias,
    dec_weight,
    dec_bias,
):
    rows_here = queries.shape[0]
    att_width = queries.shape[1]
    data_size = lax.axis_size("dp")
    latent_size = lax.axis_size("latent")
    all_rows = rows_here * data_size * latent_size
    heads_out = attend(queries, cache_keys, cache_values, positions)
    local_energy = jnp.sum(jnp.square(heads_out.astype(jnp.float32)))
    energy = lax.psum(local_energy, ("dp", "latent"))
    norm_scale = lax.rsqrt(energy / (all_rows * att_width) + epsilon)
    moving = (heads_out.astype(jnp.float32) * norm_scale).astype(jnp.bfloat16)
    arrived = shuffle_rows(moving, shuffle)
    gathered = lax.all_gather(arrived, "latent", axis=0, tiled=True)
    start_row = lax.axis_index("latent") * rows_here
    preact = jnp.dot(gathered, enc_weight, preferred_element_type=jnp.float32) + enc_bias[None, :]
    active = jax.nn.softplus(sharpness * preact) / sharpness
    coded_half = active.astype(jnp.bfloat16)
    dec_float = dec_weight.astype(jnp.float32)
    dec_norms = jnp.sqrt(jnp.sum(jnp.square(dec_float), axis=1) + epsilon)
    partial_value = jnp.dot(coded_half, dec_weight, preferred_element_type=jnp.float32)
    summed = lax.psum(partial_value, "latent")
    rebuilt_all = summed + dec_bias[None, :]
    residual = rebuilt_all - gathered.astype(jnp.float32)
    residual_half = residual.astype(jnp.bfloat16)
    own_rebuilt = lax.dynamic_slice_in_dim(rebuilt_all, start_row, rows_here, 0)
    grad_active = (
        2.0
        / all_rows
        * lax.dot_general(
            residual_half, dec_weight, (((1,), (1,)), ((), ())), preferred_element_type=jnp.float32
        )
    )
    grad_active = grad_active + sparsity_weight / all_rows * dec_norms[None, :]
    grad_pre = (grad_active * jax.nn.sigmoid(sharpness * preact)).astype(jnp.bfloat16)
    grad_enc = lax.psum_scatter(
        lax.dot_general(
            gathered, grad_pre, (((0,), (0,)), ((), ())), preferred_element_type=jnp.float32
        ).astype(jnp.bfloat16),
        "dp",
        scatter_dimension=0,
        tiled=True,
    ).astype(jnp.float32)
    column_sums = jnp.sum(coded_half.astype(jnp.float32), axis=0)
    dec_term = (
        2.0
        / all_rows
        * lax.dot_general(
            coded_half, residual_half, (((0,), (0,)), ((), ())), preferred_element_type=jnp.float32
        )
    )
    dec_term = (
        dec_term
        + sparsity_weight / all_rows * column_sums[:, None] * dec_float / dec_norms[:, None]
    )
    grad_dec = lax.psum_scatter(
        dec_term.astype(jnp.bfloat16), "dp", scatter_dimension=1, tiled=True
    ).astype(jnp.float32)
    return (own_rebuilt.astype(jnp.bfloat16), grad_enc, grad_dec)


def solution(mesh):
    in_specs = (
        P(("dp", "latent"), None),
        P(("dp", "latent"), None, None),
        P(("dp", "latent"), None, None),
        P(("dp", "latent")),
        P(("dp", "latent")),
        P(None, "latent"),
        P("latent"),
        P("latent", None),
        P(),
    )
    out_specs = (P(("dp", "latent"), None), P("dp", "latent"), P("latent", "dp"))
    return jax.shard_map(shards, mesh=mesh, in_specs=in_specs, out_specs=out_specs, check_vma=False)
```

profile of v0, /device:TPU:32, one launch (start us, length us, event | category | flops | bytes accessed | tf_op | source)
XLA Modules:
  0.0 480.0 jit_solution(15910720010566987402)
XLA Ops:
  7.2 0.8 and_select_fusion
  7.9 1.6 sort.34
  9.5 1.4 gather_fusion.1
  11.0 0.6 add_select_fusion
  11.6 7.0 %all-to-all-start.1 = ((s32[16,1,2]{2,1,0:T(1,128)}), s32[16,1,2]{2,1,0:T(1,128)S(1)}, u32[]{:S(2)}, u32[]{:S(2)}) async-start(s32[16,1,2]{2,1,0:T(1,128)} %bitcast.3), calls=%async_computation.1 | async-start | bytes 16384 | tf_op jit(solution)/shard_map/all_to_all | solution.py:46
  18.7 1.9 reshape_squeeze.7
  20.6 0.8 reshape_squeeze.6
  22.3 1.1 multiply_reduce_fusion
  23.4 79.0 %psum.14 = f32[]{:T(128)} all-reduce(f32[]{:T(128)} %get-tuple-element.11), channel_id=1, replica_groups=mesh['dp'=16,'latent'=16] {'dp','latent'}, use_global_device_ids=true, to_apply=%region_3.4 | all-reduce | flops 1 | bytes 8 | tf_op jit(solution)/shard_map/psum | solution.py:71
  103.4 0.7 gather_fusion
  104.0 0.8 reshape.122
  104.8 3.5 all-to-all-start
  108.9 0.7 reduce.5
  109.7 1.6 sort.35
  111.3 4.8 %all-to-all-done = bf16[16,2,2048]{2,1,0:T(2,128)(2,1)S(1)} async-done(((bf16[16,2,2048]{2,1,0:T(2,128)(2,1)}), bf16[16,2,2048]{2,1,0:T(2,128)(2,1)S(1)}, u32[]{:S(2)}, u32[]{:S(2)}) %all-to-all-start) | async-done | bytes 131104 | tf_op jit(solution)/shard_map/all_to_all | solution.py:45
  116.2 1.3 gather_fusion.2
  117.5 34.9 %all-gather.3.cloned.1.call-done = bf16[512,2048]{1,0:T(8,128)(2,1)} async-done(((bf16[32,2048]{1,0:T(8,128)(2,1)}), bf16[512,2048]{1,0:T(8,128)(2,1)}) %all-gather.3.cloned.1.call-update) | async-done | bytes 2097168 | tf_op jit(solution)/shard_map/all_gather | solution.py:75
  152.5 7.7 %convert_reduce_fusion = (f32[1024]{0:T(1024)S(1)}, bf16[512,1024]{1,0:T(8,128)(2,1)S(1)}, f32[512,1024]{1,0:T(8,128)}) fusion(f32[1024]{0:T(1024)S(1)} %copy-done.8, bf16[512,2048]{1,0:T(8,128)(2,1)} %all-gather.3.cloned.1.call-done, bf16[2048,1024]{1,0:T(8,128)(2,1)} %param.14), kind=kOutput, calls=%fused_computation.15 | convolution fusion | flops 2153774080 | bytes 9445376 | tf_op jit(solution)/shard_map/dot_general | solution.py:77
  160.2 4.3 fusion.23
  164.8 3.1 fusion.1
  167.9 114.6 %all-reduce.2.cloned.1.call-done = f32[512,2048]{1,0:T(8,128)} async-done(((f32[512,2048]{1,0:T(8,128)}), f32[512,2048]{1,0:T(8,128)}) %all-reduce.2.cloned.1.call-update) | async-done | bytes 4194320 | tf_op jit(solution)/shard_map/psum | solution.py:83
  282.5 2.8 broadcast_add_fusion
  285.3 1.9 copy-done
  287.2 5.1 %fusion.4 = bf16[1024,2048]{1,0:T(8,128)(2,1)} fusion(bf16[1024,2048]{1,0:T(8,128)(2,1)S(1)} %copy-done.2, bf16[512,1024]{1,0:T(8,128)(2,1)S(1)} %get-tuple-element.8, f32[1024]{0:T(1024)S(1)} %get-tuple-element.9, f32[1024]{0:T(1024)S(1)} %broadcast_multiply_fusion, f32[512,2048]{1,0:T(8,128)S(1)} %broadcast_add_fusion, bf16[512,2048]{1,0:T(8,128)(2,1)S(1)} %copy-done.7), kind=kOutput, calls=%fused_computation.9 | convolution fusion | flops 2163212288 | bytes 15736832 | tf_op jit(solution)/shard_map/dot_general | solution.py:109
  292.4 6.4 %copy.30 = bf16[1024,2048]{0,1:T(8,128)(2,1)} copy(bf16[1024,2048]{1,0:T(8,128)(2,1)} %fusion.4) | data formatting | bytes 8388608
  298.9 10.9 %convolution_convert_fusion = bf16[2048,1024]{1,0:T(8,128)(2,1)} fusion(bf16[512,2048]{1,0:T(8,128)(2,1)S(1)} %copy-done.7, f32[512,1024]{1,0:T(8,128)} %get-tuple-element.13, bf16[1024,2048]{1,0:T(8,128)(2,1)} %param.16, f32[1024]{0:T(1024)S(1)} %get-tuple-element.10, f32[1024]{0:T(1024)S(1)} %copy-done.8, f32[512,2048]{1,0:T(8,128)} %copy-done), kind=kOutput, calls=%fused_computation.12 | convolution fusion | flops 4304928768 | bytes 16785408 | tf_op jit(solution)/shard_map/dot_general | solution.py:98
  309.8 1.6 dynamic-slice_convert_fusion
  311.4 73.9 %reduce-scatter.7.cloned.1.call-done = bf16[128,1024]{1,0:T(8,128)(2,1)} async-done(((bf16[2048,1024]{1,0:T(8,128)(2,1)}), bf16[128,1024]{1,0:T(8,128)(2,1)}) %reduce-scatter.7.cloned.1.call-update) | async-done | bytes 262160
  385.3 1.1 copy.31
  386.4 0.8 convert_element_type.69
  387.3 84.4 %reduce-scatter.5.cloned.1.call-done = bf16[128,1024]{1,0:T(8,128)(2,1)} async-done(((bf16[2048,1024]{1,0:T(8,128)(2,1)}), bf16[128,1024]{1,0:T(8,128)(2,1)}) %reduce-scatter.5.cloned.1.call-update) | async-done | bytes 262160 | tf_op jit(solution)/shard_map/reduce_scatter | solution.py:97
  471.7 1.8 convert_element_type.66
  (45 shorter events, 2.3 us)
Async XLA Ops:
  7.2 13.4 %copy-start.3 = (bf16[1,512,1024]{2,1,0:T(8,128)(2,1)S(1)}, bf16[1,512,1024]{2,1,0:T(8,128)(2,1)}, u32[]{:S(2)}) copy-start(bf16[1,512,1024]{2,1,0:T(8,128)(2,1)} %param.10) | copy-start | bytes 3145732
  11.6 93.2 %all-to-all-start.1 = ((s32[16,1,2]{2,1,0:T(1,128)}), s32[16,1,2]{2,1,0:T(1,128)S(1)}, u32[]{:S(2)}, u32[]{:S(2)}) async-start(s32[16,1,2]{2,1,0:T(1,128)} %bitcast.3), calls=%async_computation.1 | async-start | bytes 16384 | tf_op jit(solution)/shard_map/all_to_all | solution.py:46
  18.7 2.7 copy-start.6
  18.7 2.8 copy-start.4
  103.1 49.3 %copy-start.8 = (f32[1024]{0:T(1024)S(1)}, f32[1024]{0:T(1024)}, u32[]{:S(2)}) copy-start(f32[1024]{0:T(1024)} %param.15) | copy-start | bytes 12292
  104.8 11.3 %all-to-all-start = ((bf16[16,2,2048]{2,1,0:T(2,128)(2,1)}), bf16[16,2,2048]{2,1,0:T(2,128)(2,1)S(1)}, u32[]{:S(2)}, u32[]{:S(2)}) async-start(bf16[16,2,2048]{2,1,0:T(2,128)(2,1)} %reshape.122), calls=%async_computation | async-start | bytes 262144 | tf_op jit(solution)/shard_map/all_to_all | solution.py:45
  108.3 44.1 %all-gather.3.cloned.1.call-start = ((), (), s32[]{:S(2)}) async-start(), calls=%async_computation.6 | async-start | bytes 2228224 | tf_op jit(solution)/shard_map/all_gather | solution.py:75
  117.5 165.0 %all-reduce.2.cloned.1.call-start = ((), (), s32[]{:S(2)}) async-start(), calls=%async_computation.4 | async-start | bytes 8388608 | tf_op jit(solution)/shard_map/psum | solution.py:83
  152.5 7.7 %copy-start.1 = (bf16[1024,2048]{1,0:T(8,128)(2,1)S(1)}, bf16[1024,2048]{1,0:T(8,128)(2,1)}, u32[]{:S(2)}) copy-start(bf16[1024,2048]{1,0:T(8,128)(2,1)} %param.16) | copy-start | bytes 12582916
  164.6 117.9 %copy-start.5 = (f32[2048]{0:T(1024)S(1)}, f32[2048]{0:T(1024)}, u32[]{:S(2)}) copy-start(f32[2048]{0:T(1024)} %param.17) | copy-start | bytes 24580
  164.6 220.7 %reduce-scatter.7.cloned.1.call-start = ((), (), s32[]{:S(2)}) async-start(), calls=%async_computation.7 | async-start | bytes 4456448
  167.9 119.3 %copy-start.7 = (bf16[512,2048]{1,0:T(8,128)(2,1)S(1)}, bf16[512,2048]{1,0:T(8,128)(2,1)}, u32[]{:S(2)}) copy-start(bf16[512,2048]{1,0:T(8,128)(2,1)} %all-gather.3.cloned.1.call-done) | copy-start | bytes 6291460
  282.5 4.7 copy-start.2
  285.3 1.9 copy-start
  298.8 172.9 %reduce-scatter.5.cloned.1.call-start = ((), (), s32[]{:S(2)}) async-start(), calls=%async_computation.5 | async-start | bytes 4456448 | tf_op jit(solution)/shard_map/reduce_scatter | solution.py:97
Sparse Core Ops, SparseCore 0:
  117.6 34.8 all-gather.2
  164.7 117.7 all-reduce.1
  298.9 86.3 reduce-scatter.6
  388.8 82.8 reduce-scatter.4
where the time goes:
time: 481 us; the launch traced here: 480 us
  waiting for transfers between devices  313 us (65%)
  blocking collectives  79 us (16%)
  matrix products  29.7 us (6%)
  local copies, waits for them, and re-layouts  18.9 us (4%)
  between operations  14.7 us (3%)
  other arithmetic  14.1 us (3%)
  starting transfers between devices  10.9 us (2%)
    psum x1, waiting for transfers between devices, shards(): summed = lax.psum(partial_value, 'latent')  115 us
    reduce_scatter x1, waiting for transfers between devices, shards(): lax.psum_scatter(lax.dot_general(gathered, grad_pre, (((0,), (0,)), ((),...  84.4 us
    psum x1, blocking collectives, shards(): energy = lax.psum(local_energy, ('dp', 'latent'))  79 us
    unnamed x5, waiting for transfers between devices  74 us
    all_gather x1, waiting for transfers between devices, shards(): gathered = lax.all_gather(arrived, 'latent', axis=0, tiled=True)  34.9 us
    dot_general x1, matrix products, shards(): lax.dot_general(gathered, grad_pre, (((0,), (0,)), ((), ())), preferred_e...  10.9 us
  transfers between devices with their start and end apart: 6, of which 5 were waited for; matrix products, arithmetic and copies ran while one was open for 6% of the time, Pallas kernels for 0%

commit v1 on v0

v1 whole, which is shorter than its diff:
```python
import jax
import jax.numpy as jnp
from jax import lax
from jax.experimental import pallas as pl
from jax.experimental.pallas import tpu as pltpu
from jax.sharding import PartitionSpec as P

F32 = jnp.float32
BF16 = jnp.bfloat16
MESH = pl.DeviceIdType.MESH

HEAD_DIM = 256
KV_HEADS = 4
HEADS = 8
CACHE = 512
ROWS_DEV = 32
GROUP = 512
WIDTH = 2048
LAT = 1024
ALL_ROWS = 8192
N_X = 4
N_Z = 8
N_DP = 16
CHUNKS = 4
COLS = WIDTH // CHUNKS
EPSILON = 1e-06
GRAD_SCALE = 2.0 / ALL_ROWS
SPARSE_SCALE = 1.0 / ALL_ROWS

N_SEMS = 264


def dot(a, b):
    return jnp.dot(a, b, preferred_element_type=F32)


def dot_nt(a, b):
    return lax.dot_general(a, b, (((1,), (1,)), ((), ())), preferred_element_type=F32)


def iota(shape, axis):
    return lax.broadcasted_iota(jnp.int32, shape, axis)


def chunk_dp(j, s):
    return s * N_X + (j - s) % N_X


def kernel(
    queries, keys, values, positions, shuffle, enc_w, enc_bias, dec_w, dec_bias,
    rebuilt_out, enc_out, dec_out,
    q_v, k_v, v_v, enc_v, dec_v, heads, outgoing, arrived, notes_out, notes_in,
    energies, gathered, inputs, batch, inputs_t, coded, coded_t, gate, norm_row, dec_coef,
    part_send, part_recv, part_own, rs_send_p, rs_recv_p, rs_send_m, rs_recv_m,
    residual, grad_act, grad_pre, dec_term, enc_term,
    dec_r1, dec_r2, enc_r1, enc_r2, dec_u, enc_u, dec_s1, dec_s2, enc_s1, enc_s2,
    send_sems, recv_sems, local_sems,
):
    me_dp = lax.axis_index("dp")
    me_l = lax.axis_index("latent")
    x, y = me_dp // N_X, me_dp % N_X
    z, core = me_l // 2, me_l % 2
    other = 1 - core

    def at_z(k):
        return {"latent": lax.rem(z + k + N_Z, N_Z) * 2 + core}

    partner = {"latent": z * 2 + other}

    def at_x(k):
        return {"dp": lax.rem(x + k + N_X, N_X) * N_X + y}

    def at_y(k):
        return {"dp": x * N_X + lax.rem(y + k + N_X, N_X)}

    counter = [0]
    sent = []

    def remote(src, dst, device):
        i = counter[0]
        counter[0] += 1
        return pltpu.make_async_remote_copy(
            src_ref=src, dst_ref=dst, send_sem=send_sems.at[i], recv_sem=recv_sems.at[i],
            device_id=device, device_id_type=MESH,
        )

    def start(copy):
        copy.start()
        sent.append(copy)
        return copy

    def load(src, dst, i):
        c = pltpu.make_async_copy(src, dst, local_sems.at[i])
        c.start()
        return c

    load_q = load(queries, q_v, 0)
    load_k = load(keys.at[0], k_v, 1)
    load_v = load(values.at[0], v_v, 2)
    load_e = load(enc_w, enc_v, 3)
    load_d = []
    for j in range(CHUNKS):
        for s in range(N_X):
            d = chunk_dp(j, s)
            load_d.append(
                load(dec_w.at[:, d * 128:(d + 1) * 128], dec_v.at[j, :, s * 128:(s + 1) * 128], 4 + j * N_X + s)
            )

    barrier = pltpu.get_barrier_semaphore()
    for o in range(1, N_DP):
        pl.semaphore_signal(barrier, inc=1, device_id={"dp": lax.rem(me_dp + o, N_DP)}, device_id_type=MESH)
        pl.semaphore_signal(barrier, inc=1, device_id={"latent": lax.rem(me_l + o, N_DP)}, device_id_type=MESH)

    shuffle_row = shuffle[...]
    sub = iota((ROWS_DEV, ROWS_DEV), 0)
    lane = iota((ROWS_DEV, ROWS_DEV), 1)
    eye = sub == lane
    wide = jnp.broadcast_to(shuffle_row, (ROWS_DEV, ROWS_DEV))
    shuffle_col = jnp.sum(jnp.where(eye, wide.astype(F32), 0.0), axis=1, keepdims=True).astype(jnp.int32)
    target_row = lax.shift_right_logical(wide, 9)
    target_col = lax.shift_right_logical(shuffle_col, 9)
    before = jnp.where((target_row == target_col) & (lane < sub), 1.0, 0.0)
    slot_col = 2.0 * target_col.astype(F32) + jnp.sum(before, axis=1, keepdims=True)
    lane_w = iota((ROWS_DEV, 256), 1)
    sub_w = iota((ROWS_DEV, 256), 0)
    slot_wide = jnp.sum(
        jnp.where((lane_w & 31) == sub_w, jnp.broadcast_to(slot_col, (ROWS_DEV, 256)), 0.0), axis=0, keepdims=True
    ).astype(jnp.int32)
    slot_row = jnp.sum(jnp.where(eye, jnp.broadcast_to(slot_col, (ROWS_DEV, ROWS_DEV)), 0.0), axis=0, keepdims=True)
    slot_row = slot_row.astype(jnp.int32)
    place_row = (shuffle_row & 31).astype(F32)
    sub_q = iota((256, 256), 0)
    lane_q = iota((256, 256), 1)
    pick = (sub_q & 7) == lax.shift_right_logical(lane_q, 5)
    pick = pick & (lax.shift_right_logical(sub_q, 3) == slot_wide)
    pick = jnp.where(pick, 1.0, 0.0).astype(BF16)

    pos_wide = jnp.broadcast_to(positions[...], (ROWS_DEV, ROWS_DEV)).astype(F32)
    pos_col = jnp.sum(jnp.where(eye, pos_wide, 0.0), axis=1, keepdims=True).astype(jnp.int32)
    pos_col = jnp.concatenate([pos_col, pos_col], axis=0)
    visible = iota((2 * ROWS_DEV, CACHE), 1) <= pos_col
    load_q.wait()
    load_k.wait()
    load_v.wait()
    energy = jnp.zeros((1, 1), F32)
    for g in range(KV_HEADS):
        cols = slice(g * HEAD_DIM, (g + 1) * HEAD_DIM)
        pair = jnp.concatenate(
            [q_v[:, (2 * g + i) * HEAD_DIM:(2 * g + i + 1) * HEAD_DIM] for i in range(2)], axis=0
        )
        scores = dot_nt(pair, k_v[:, cols]) * HEAD_DIM ** (-0.5)
        scores = jnp.where(visible, scores, -jnp.inf)
        weights = jnp.exp(scores - jnp.max(scores, axis=1, keepdims=True))
        probs = (weights / jnp.sum(weights, axis=1, keepdims=True)).astype(BF16)
        mixed = dot(probs, v_v[:, cols]).astype(BF16)
        heads[g * 64:(g + 1) * 64, :] = mixed
        square = jnp.square(mixed.astype(F32))
        energy = energy + jnp.sum(jnp.sum(square, axis=1, keepdims=True), axis=0, keepdims=True)
    outgoing[...] = dot(pick, heads[...]).astype(BF16)

    note_sub = iota((128, 256), 0)
    note_lane = iota((128, 256), 1)
    peer_sub = lax.shift_right_logical(iota((128, ROWS_DEV), 0), 3)
    slot_n = jnp.broadcast_to(slot_row, (128, ROWS_DEV))
    place_n = jnp.broadcast_to(place_row, (128, ROWS_DEV))
    place = [
        jnp.sum(jnp.where(slot_n == 2 * peer_sub + k, place_n, 0.0), axis=1, keepdims=True) for k in range(2)
    ]
    mine = lax.shift_right_logical(note_lane, 4) == me_dp
    place_note = jnp.where((lax.shift_right_logical(note_lane, 3) & 1) == 0, place[0], place[1])
    place_note = jnp.where(mine, place_note, 0.0)
    notes_out[...] = jnp.where((note_sub & 7) == 0, place_note, jnp.broadcast_to(energy, (128, 256)))

    pl.semaphore_wait(barrier, 2 * (N_DP - 1))
    own16 = pl.ds(pl.multiple_of(me_dp * 16, 16), 16)
    own8 = pl.ds(pl.multiple_of(me_dp * 8, 8), 8)
    waits = []
    for o in range(1, N_DP):
        to = lax.rem(me_dp + o, N_DP)
        frm = lax.rem(me_dp + N_DP - o, N_DP)
        to16 = pl.ds(pl.multiple_of(to * 16, 16), 16)
        to8 = pl.ds(pl.multiple_of(to * 8, 8), 8)
        frm16 = pl.ds(pl.multiple_of(frm * 16, 16), 16)
        frm8 = pl.ds(pl.multiple_of(frm * 8, 8), 8)
        for src, dst, to_at, own_at, frm_at in (
            (outgoing, arrived, to16, own16, frm16),
            (notes_out, notes_in, to8, own8, frm8),
        ):
            i = counter[0]
            c = start(remote(src.at[to_at], dst.at[own_at], {"dp": to}))
            waits.append(
                pltpu.make_async_remote_copy(
                    src_ref=src.at[to_at], dst_ref=dst.at[frm_at], send_sem=send_sems.at[i],
                    recv_sem=recv_sems.at[i], device_id={"dp": to}, device_id_type=MESH,
                )
            )
    arrived[own16, :] = outgoing[own16, :]
    notes_in[own8, :] = notes_out[own8, :]
    for c in waits:
        c.wait_recv()
    note = notes_in[0:8, :]
    for s in range(1, N_DP):
        note = note + notes_in[s * 8:(s + 1) * 8, :]
    place_q = jnp.broadcast_to(note[0:1, :], (256, 256)).astype(jnp.int32)
    put = lax.shift_right_logical(sub_q, 5) == (lane_q & 7)
    put = put & ((sub_q & 31) == place_q)
    placed = dot(jnp.where(put, 1.0, 0.0).astype(BF16), arrived[...]).astype(BF16)

    def block(zb, cb, offset=0, size=ROWS_DEV):
        return pl.ds(pl.multiple_of((cb * N_Z + zb) * ROWS_DEV + offset, 16), size)

    def chip(k):
        return lax.rem(z + k + N_Z, N_Z)

    own = block(z, core)
    for h in range(HEADS):
        gathered[own, h * 256:(h + 1) * 256] = placed[h * 32:(h + 1) * 32, :]
    tile = jnp.broadcast_to(note[1:2, 0:128], (8, 128))
    energies[me_l] = tile

    def gather_events(buf, pieces):
        size = ROWS_DEV // pieces
        half = ROWS_DEV // 2
        plan = {}
        for sign in (1, -1):
            for k in range(1, 5):
                if k < 4:
                    parts = [(p * size, size) for p in range(pieces)]
                else:
                    parts = [(0 if sign == 1 else half, half)]
                for off, sz in parts:
                    src_z = chip(-sign * (k - 1))
                    ref = buf.at[block(src_z, core, off, sz)]
                    got = chip(-sign * k)
                    copy = remote(ref, ref, at_z(sign))
                    got_ref = buf.at[block(got, core, off, sz)]
                    arrival = pltpu.make_async_remote_copy(
                        src_ref=got_ref, dst_ref=got_ref, send_sem=send_sems.at[counter[0] - 1],
                        recv_sem=recv_sems.at[counter[0] - 1], device_id=at_z(sign), device_id_type=MESH,
                    )
                    pass_on = remote(got_ref, got_ref, partner)
                    other_ref = buf.at[block(got, other, off, sz)]
                    passed = pltpu.make_async_remote_copy(
                        src_ref=other_ref, dst_ref=other_ref, send_sem=send_sems.at[counter[0] - 1],
                        recv_sem=recv_sems.at[counter[0] - 1], device_id=partner, device_id_type=MESH,
                    )
                    plan[(sign, k, off)] = (copy, arrival, pass_on, passed, sz)
        own_ref = buf.at[own]
        own_pass = remote(own_ref, own_ref, partner)
        own_other = buf.at[block(z, other)]
        own_passed = pltpu.make_async_remote_copy(
            src_ref=own_other, dst_ref=own_other, send_sem=send_sems.at[counter[0] - 1],
            recv_sem=recv_sems.at[counter[0] - 1], device_id=partner, device_id_type=MESH,
        )

        def first():
            for p in range(pieces):
                for sign in (1, -1):
                    start(plan[(sign, 1, p * size)][0])
            start(own_pass)

        def step(k):
            offs = [p * size for p in range(pieces)]
            for n in range(pieces):
                for sign in (1, -1):
                    if k < 4:
                        off = offs[n] if sign == 1 else offs[pieces - 1 - n]
                        off = offs[n]
                    else:
                        if n > 0:
                            continue
                        off = 0 if sign == 1 else half
                    copy, arrival, pass_on, passed, sz = plan[(sign, k, off)]
                    arrival.wait_recv()
                    if k < 3:
                        start(plan[(sign, k + 1, off)][0])
                    elif k == 3:
                        wanted = 0 if sign == 1 else half
                        if pieces == 1 or off == wanted:
                            start(plan[(sign, 4, wanted)][0])
                    start(pass_on)

        def finish(k):
            if k == 0:
                own_passed.wait_recv()
                return
            for key, item in plan.items():
                if key[1] == abs(k) and (abs(k) == 4 or key[0] == (1 if k > 0 else -1)):
                    item[3].wait_recv()

        return first, step, finish

    first, step, finish = gather_events(gathered, 2)
    first()
    e_waits = []
    for o in range(1, N_DP):
        to = lax.rem(me_l + o, N_DP)
        frm = lax.rem(me_l + N_DP - o, N_DP)
        i = counter[0]
        start(remote(energies.at[me_l], energies.at[me_l], {"latent": to}))
        e_waits.append(
            pltpu.make_async_remote_copy(
                src_ref=energies.at[me_l], dst_ref=energies.at[frm], send_sem=send_sems.at[i],
                recv_sem=recv_sems.at[i], device_id={"latent": to}, device_id_type=MESH,
            )
        )

    for c in load_d:
        c.wait()
    diag = iota((128, 128), 0) == iota((128, 128), 1)
    norms = []
    for b in range(LAT // 128):
        total = jnp.zeros((128, 1), F32)
        for j in range(CHUNKS):
            total = total + jnp.sum(jnp.square(dec_v[j, b * 128:(b + 1) * 128, :].astype(F32)), axis=1, keepdims=True)
        norm = jnp.sqrt(total + EPSILON)
        norms.append(norm)
        norm_row[0:1, b * 128:(b + 1) * 128] = SPARSE_SCALE * jnp.sum(
            jnp.where(diag, jnp.broadcast_to(norm, (128, 128)), 0.0), axis=0, keepdims=True
        )
        dec_coef[b * 128:(b + 1) * 128, :] = jnp.broadcast_to(SPARSE_SCALE / norm, (128, 128))

    for c in e_waits:
        c.wait_recv()
    total = energies[0]
    for s in range(1, N_DP):
        total = total + energies[s]
    norm_scale = lax.rsqrt(total[0:1, 0:1] / (ALL_ROWS * WIDTH) + EPSILON)

    load_e.wait()

    def encode(chips):
        spots = [block(zb, cb) for zb in chips for cb in range(2)]
        for n, spot in enumerate(spots):
            scaled = (gathered[spot, :].astype(F32) * norm_scale).astype(BF16)
            inputs[spot, :] = scaled
            batch[n * ROWS_DEV:(n + 1) * ROWS_DEV, :] = scaled

        def tile_step(t, carry):
            at = pl.ds(pl.multiple_of(t * 256, 256), 256)
            pre = 4.0 * (dot(batch[...], enc_v[:, at]) + enc_bias[:, at])
            small = jnp.exp(-jnp.abs(pre))
            active = 0.25 * (jnp.maximum(pre, 0.0) + jnp.log1p(small))
            sig = jnp.where(pre >= 0, 1.0, small) / (1.0 + small)
            act = active.astype(BF16)
            for n, spot in enumerate(spots):
                part = slice(n * ROWS_DEV, (n + 1) * ROWS_DEV)
                coded[spot, at] = act[part, :]
                gate[spot, at] = sig[part, :]
            return carry

        lax.fori_loop(0, LAT // 256, tile_step, 0)

    step(1)
    finish(0)
    finish(1)
    encode((z, chip(-1)))
    step(2)
    finish(-1)
    finish(2)
    encode((chip(1), chip(-2)))
    step(3)
    finish(-2)
    finish(3)
    encode((chip(2), chip(-3)))
    step(4)
    finish(-3)
    finish(4)
    encode((chip(3), chip(4)))

    events = []

    def at_time(t, fn):
        events.append((t, len(events), fn))

    own_half = pl.ds(pl.multiple_of(core * 256, 256), 256)
    other_half = pl.ds(pl.multiple_of(other * 256, 256), 256)
    STEP = 2.3

    def transpose_coded(b):
        def run():
            turned = coded[:, b * 256:(b + 1) * 256].T
            coded_t[b * 256:(b + 1) * 256, :] = turned
            sums = jnp.sum(turned.astype(F32), axis=1, keepdims=True)
            dec_coef[b * 256:(b + 1) * 256, :] = dec_coef[b * 256:(b + 1) * 256, :] * sums
        return run

    def transpose_inputs(j):
        def run():
            for s in range(N_X):
                d = chunk_dp(j, s)
                inputs_t[j, s * 128:(s + 1) * 128, :] = inputs[:, d * 128:(d + 1) * 128].T
        return run

    for b in range(4):
        at_time(5.0 + 2.4 * b, transpose_coded(b))
        at_time(6.2 + 2.4 * b, transpose_inputs(b))

    def latent_stream(j):
        base = 1.0 * j
        swap = remote(part_send.at[j], part_recv.at[j], partner)

        def start_half():
            part_send[j] = dot(coded[other_half, :], dec_v[j]).astype(BF16)
            start(swap)

        def own_part():
            part_own[j] = dot(coded[own_half, :], dec_v[j])

        ring = {}
        for sign, out_buf, in_buf in ((1, rs_send_p, rs_recv_p), (-1, rs_send_m, rs_recv_m)):
            for t in range(4):
                if t == 0:
                    rows = slice(0, 16) if sign == 1 else slice(16, 32)
                else:
                    rows = slice(0, 32)
                ring[(sign, t)] = remote(out_buf.at[j, t, rows], in_buf.at[j, t, rows], at_z(sign))

        def own_block(zb):
            rows = pl.ds(pl.multiple_of(zb * ROWS_DEV, ROWS_DEV), ROWS_DEV)
            return part_own[j, rows, :] + part_recv[j, rows, :].astype(F32)

        def reduce_step(t):
            def run():
                if t == 0:
                    swap.wait_recv()
                for sign, out_buf, in_buf in ((1, rs_send_p, rs_recv_p), (-1, rs_send_m, rs_recv_m)):
                    mine_ = own_block(chip(sign * (4 - t)))
                    near = slice(0, 16) if sign == 1 else slice(16, 32)
                    far = slice(16, 32) if sign == 1 else slice(0, 16)
                    if t == 0:
                        out_buf[j, 0, near, :] = mine_[near, :].astype(BF16)
                    else:
                        ring[(sign, t - 1)].wait_recv()
                        if t == 1:
                            out_buf[j, 1, near, :] = (mine_[near, :] + in_buf[j, 0, near, :].astype(F32)).astype(BF16)
                            out_buf[j, 1, far, :] = mine_[far, :].astype(BF16)
                        else:
                            out_buf[j, t, :, :] = (mine_ + in_buf[j, t - 1, :, :].astype(F32)).astype(BF16)
                    start(ring[(sign, t)])
            return run

        first_, step_, finish_ = gather_events(residual.at[j], 1)

        def own_sum():
            ring[(1, 3)].wait_recv()
            ring[(-1, 3)].wait_recv()
            summed = own_block(z) + rs_recv_p[j, 3, :, :].astype(F32) + rs_recv_m[j, 3, :, :].astype(F32)
            spans = [slice(chunk_dp(j, s) * 128, chunk_dp(j, s) * 128 + 128) for s in range(N_X)]
            bias = jnp.concatenate([dec_bias[:, sp] for sp in spans], axis=1)
            rebuilt = summed + bias
            rebuilt_half = rebuilt.astype(BF16)
            for s, sp in enumerate(spans):
                rebuilt_out[:, sp] = rebuilt_half[:, s * 128:(s + 1) * 128]
            ins = jnp.concatenate([inputs[own, sp] for sp in spans], axis=1).astype(F32)
            residual[j, own, :] = (rebuilt - ins).astype(BF16)
            first_()

        at_time(base, start_half)
        at_time(base + 0.5, own_part)
        for t in range(4):
            at_time(base + 2.5 + t * STEP, reduce_step(t))
        at_time(base + 2.5 + 4 * STEP, own_sum)
        for k in range(1, 5):
            at_time(base + 2.5 + (4 + k) * STEP, lambda k=k: step_(k))

        def all_in():
            finish_(0)
            for k in (1, -1, 2, -2, 3, -3, 4):
                finish_(k)

        return base + 2.5 + 8 * STEP + 1.0, all_in

    def pair_reduce(pick_ref, split, first_in, second_in, hop, me):
        a, b = (0, split), (split, split)
        far = lax.rem(me + 2, N_X)
        up, down = lax.rem(me + 1, N_X), lax.rem(me + 3, N_X)
        full = (0, 2 * split)
        far_up = remote(pick_ref(far, a), first_in.at[0], hop(1))
        far_down = remote(pick_ref(far, b), first_in.at[1], hop(-1))
        near_up = remote(pick_ref(up, full), second_in.at[0], hop(1))
        near_down = remote(pick_ref(down, full), second_in.at[1], hop(-1))

        def go():
            start(far_up)
            start(far_down)

        def combine():
            for copy, place_, part, ref, nxt in (
                (far_up, up, a, first_in.at[0], near_up),
                (far_down, down, b, first_in.at[1], near_down),
            ):
                copy.wait_recv()
                spot = pick_ref(place_, part)
                spot[...] = (spot[...].astype(F32) + ref[...].astype(F32)).astype(BF16)
                start(nxt)

        def total():
            near_up.wait_recv()
            near_down.wait_recv()
            spot = pick_ref(me, full)
            return spot[...].astype(F32) + second_in[0].astype(F32) + second_in[1].astype(F32)

        return go, combine, total

    def grad_stream(term, halves, r1, r2, u, s1, s2, out, rows):
        half = rows // 2
        split = half // 2
        parts = []
        for j in range(CHUNKS):
            both = []
            for o in range(2):
                me = x if o == 0 else y
                hop = at_x if o == 0 else at_y

                def pick_ref(i, part, j=j, o=o):
                    s = i if o == 0 else lax.rem(j - i + N_X, N_X)
                    return term.at[j, s, pl.ds(o * half + part[0], part[1])]

                both.append(pair_reduce(pick_ref, split, r1.at[j, o], r2.at[j, o], hop, me))
            parts.append(both)
        tail = []
        for o in range(2):
            me = y if o == 0 else x
            hop = at_y if o == 0 else at_x

            def pick_ref(i, part, o=o):
                j = lax.rem(i + (x if o == 0 else y), N_X)
                return u.at[o, j, pl.ds(part[0], part[1])]

            tail.append(pair_reduce(pick_ref, split, s1.at[o], s2.at[o], hop, me))

        def fold(j):
            def run():
                for o in range(2):
                    u[o, j] = parts[j][o][2]().astype(BF16)
            return run

        def go(j):
            for o in range(2):
                parts[j][o][0]()

        def combine(j):
            def run():
                for o in range(2):
                    parts[j][o][1]()
            return run

        def tail_go():
            for o in range(2):
                tail[o][0]()

        def tail_combine():
            for o in range(2):
                tail[o][1]()

        def tail_total():
            for o in range(2):
                out[o * half:(o + 1) * half, :] = tail[o][2]()

        return go, combine, fold, tail_go, tail_combine, tail_total

    dec_go, dec_combine, dec_fold, dec_tail_go, dec_tail_combine, dec_tail_total = grad_stream(
        dec_term, None, dec_r1, dec_r2, dec_u, dec_s1, dec_s2, dec_out, LAT
    )
    enc_go, enc_combine, enc_fold, enc_tail_go, enc_tail_combine, enc_tail_total = grad_stream(
        enc_term, None, enc_r1, enc_r2, enc_u, enc_s1, enc_s2, enc_out, 128
    )

    def dec_grad(j):
        def run():
            def tile_step(t, carry):
                at = pl.ds(pl.multiple_of(t * 256, 256), 256)
                term = GRAD_SCALE * dot(coded_t[at, :], residual[j])
                coef = dec_coef[at, :]
                for s in range(N_X):
                    sp = slice(s * 128, (s + 1) * 128)
                    dec_term[j, s, at, :] = (term[:, sp] + coef * dec_v[j, at, sp].astype(F32)).astype(BF16)
                return carry

            lax.fori_loop(0, LAT // 256, tile_step, 0)
            dec_go(j)
        return run

    def act_grad(j):
        def run():
            def tile_step(t, carry):
                at = pl.ds(pl.multiple_of(t * 256, 256), 256)
                part = dot_nt(residual[j], dec_v[j, at, :])
                if j == 0:
                    grad_act[:, at] = part
                elif j < CHUNKS - 1:
                    grad_act[:, at] = grad_act[:, at] + part
                else:
                    whole = GRAD_SCALE * (grad_act[:, at] + part) + norm_row[0:1, at]
                    grad_pre[:, at] = (whole * gate[:, at]).astype(BF16)
                return carry

            lax.fori_loop(0, LAT // 256, tile_step, 0)
        return run

    def enc_grad(j):
        def run():
            def tile_step(t, carry):
                at = pl.ds(pl.multiple_of(t * 256, 256), 256)
                term = dot(inputs_t[j], grad_pre[:, at]).astype(BF16)
                for s in range(N_X):
                    enc_term[j, s, :, at] = term[s * 128:(s + 1) * 128, :]
                return carry

            lax.fori_loop(0, LAT // 256, tile_step, 0)
            enc_go(j)
        return run

    WIRE = 4.2
    ready = 0.0
    for j in range(CHUNKS):
        t, all_in = latent_stream(j)
        ready = max(t, ready + 2.0)
        at_time(ready, all_in)
        at_time(ready + 0.1, dec_grad(j))
        at_time(ready + 0.2, act_grad(j))
        at_time(ready + 4.5, dec_combine(j))
        at_time(ready + 9.0, dec_fold(j))
    dec_end = ready + 9.0
    enc_start = ready + 2.0
    for j in range(CHUNKS):
        t = enc_start + 1.0 * j
        at_time(t, enc_grad(j))
        at_time(t + 5.0 + (WIRE - 1.0) * j, enc_combine(j))
        at_time(t + 9.5 + (WIRE - 1.0) * j, enc_fold(j))
    enc_end = enc_start + 9.5 + WIRE * 3
    at_time(dec_end + 0.1, dec_tail_go)
    at_time(dec_end + 5.0, dec_tail_combine)
    at_time(dec_end + 12.0, dec_tail_total)
    at_time(enc_end + 0.1, enc_tail_go)
    at_time(enc_end + 3.5, enc_tail_combine)
    at_time(enc_end + 8.0, enc_tail_total)

    for _, _, fn in sorted(events, key=lambda e: (e[0], e[1])):
        fn()
    for copy in sent:
        copy.wait_send()


def shards(
    queries, cache_keys, cache_values, positions, shuffle, enc_weight, enc_bias, dec_weight, dec_bias
):
    any_ = pl.BlockSpec(memory_space=pl.ANY)
    vmem = pl.BlockSpec(memory_space=pltpu.VMEM)
    quarter = ROWS_DEV // 2
    scratch = [
        ((ROWS_DEV, WIDTH), BF16),
        ((CACHE, KV_HEADS * HEAD_DIM), BF16),
        ((CACHE, KV_HEADS * HEAD_DIM), BF16),
        ((WIDTH, LAT), BF16),
        ((CHUNKS, LAT, COLS), BF16),
        ((256, 256), BF16),
        ((256, 256), BF16),
        ((256, 256), BF16),
        ((128, 256), F32),
        ((128, 256), F32),
        ((16, 8, 128), F32),
        ((GROUP, WIDTH), BF16),
        ((GROUP, WIDTH), BF16),
        ((128, WIDTH), BF16),
        ((CHUNKS, COLS, GROUP), BF16),
        ((GROUP, LAT), BF16),
        ((LAT, GROUP), BF16),
        ((GROUP, LAT), F32),
        ((8, LAT), F32),
        ((LAT, 128), F32),
        ((CHUNKS, 256, COLS), BF16),
        ((CHUNKS, 256, COLS), BF16),
        ((CHUNKS, 256, COLS), F32),
        ((CHUNKS, 4, ROWS_DEV, COLS), BF16),
        ((CHUNKS, 4, ROWS_DEV, COLS), BF16),
        ((CHUNKS, 4, ROWS_DEV, COLS), BF16),
        ((CHUNKS, 4, ROWS_DEV, COLS), BF16),
        ((CHUNKS, GROUP, COLS), BF16),
        ((GROUP, LAT), F32),
        ((GROUP, LAT), BF16),
        ((CHUNKS, 4, LAT, 128), BF16),
        ((CHUNKS, 4, 128, LAT), BF16),
        ((CHUNKS, 2, 2, 256, 128), BF16),
        ((CHUNKS, 2, 2, 512, 128), BF16),
        ((CHUNKS, 2, 2, 32, LAT), BF16),
        ((CHUNKS, 2, 2, 64, LAT), BF16),
        ((2, CHUNKS, 512, 128), BF16),
        ((2, CHUNKS, 64, LAT), BF16),
        ((2, 2, 256, 128), BF16),
        ((2, 2, 512, 128), BF16),
        ((2, 2, 32, LAT), BF16),
        ((2, 2, 64, LAT), BF16),
    ]
    return pl.pallas_call(
        kernel,
        out_shape=(
            jax.ShapeDtypeStruct((ROWS_DEV, WIDTH), BF16),
            jax.ShapeDtypeStruct((128, LAT), F32),
            jax.ShapeDtypeStruct((LAT, 128), F32),
        ),
        in_specs=[any_, any_, any_, vmem, vmem, any_, vmem, any_, vmem],
        out_specs=(vmem, vmem, vmem),
        scratch_shapes=[pltpu.VMEM(shape, dtype) for shape, dtype in scratch]
        + [
            pltpu.SemaphoreType.DMA((N_SEMS,)),
            pltpu.SemaphoreType.DMA((N_SEMS,)),
            pltpu.SemaphoreType.DMA((20,)),
        ],
        compiler_params=pltpu.CompilerParams(
            collective_id=0, has_side_effects=True, vmem_limit_bytes=67043328
        ),
    )(
        queries, cache_keys, cache_values, positions.reshape(1, -1), shuffle.reshape(1, -1),
        enc_weight, enc_bias.reshape(1, -1), dec_weight, dec_bias.reshape(1, -1),
    )


def solution(mesh):
    in_specs = (
        P(("dp", "latent"), None),
        P(("dp", "latent"), None, None),
        P(("dp", "latent"), None, None),
        P(("dp", "latent")),
        P(("dp", "latent")),
        P(None, "latent"),
        P("latent"),
        P("latent", None),
        P(),
    )
    out_specs = (P(("dp", "latent"), None), P("dp", "latent"), P("latent", "dp"))
    return jax.shard_map(shards, mesh=mesh, in_specs=in_specs, out_specs=out_specs, check_vma=False)
```

time: 481 us -> 134 us (0.28)
  waiting for transfers between devices: 313 us -> 0 us
  Pallas kernels: 0 us -> 128 us
  blocking collectives: 79 us -> 0 us
  matrix products: 29.7 us -> 0 us
  other arithmetic: 14.1 us -> 0 us
  between operations: 14.7 us -> 0.64 us
  local copies, waits for them, and re-layouts: 18.9 us -> 5.32 us
  starting transfers between devices: 10.9 us -> 0 us
    pallas_call x0 -> x1, Pallas kernels: none -> 128 us  [shards(): pl.pallas_call(kernel, out_shape=(jax.ShapeDtypeStruct((ROWS_DEV, WIDTH),...]
    psum x1 -> x0, waiting for transfers between devices: 115 us -> none  [shards(): summed = lax.psum(partial_value, 'latent')]
    reduce_scatter x1 -> x0, waiting for transfers between devices: 84.4 us -> none  [shards(): lax.psum_scatter(lax.dot_general(gathered, grad_pre, (((0,), (0,)), ((),...]
    psum x1 -> x0, blocking collectives: 79 us -> none  [shards(): energy = lax.psum(local_energy, ('dp', 'latent'))]
    unnamed x5 -> x0, waiting for transfers between devices: 74 us -> none
    all_gather x1 -> x0, waiting for transfers between devices: 34.9 us -> none  [shards(): gathered = lax.all_gather(arrived, 'latent', axis=0, tiled=True)]
    dot_general x6 -> x0, matrix products: 29.7 us -> none  [the longest x1 10.9 us: shards(): lax.dot_general(gathered, grad_pre, (((0,), (0,)), ((), ())), preferred_e...]
    all_to_all x2 -> x0, starting transfers between devices: 10.5 us -> none  [the longest x1 7.03 us: shuffle_rows(): lax.all_to_all(places, 'dp', split_axis=0, concat_axis=0, tiled=True)]
  transfers between devices with their start and end apart: 6 -> 0, of which waited for: 5 -> 0; matrix products, arithmetic and copies ran while one was open for 6% -> 0% of each run, Pallas kernels for 0% -> 0%
where the time goes in v1:
time: 134 us
  Pallas kernels  128 us (96%)
  local copies, waits for them, and re-layouts  5.32 us (4%)
    pallas_call x1, Pallas kernels, shards(): pl.pallas_call(kernel, out_shape=(jax.ShapeDtypeStruct((ROWS_DEV, WIDTH),...  128 us
    unnamed x3, local copies, waits for them, and re-layouts  5.32 us

profile of v1, /device:TPU:32, one launch (start us, length us, event | category | flops | bytes accessed | tf_op | source)
XLA Modules:
  0.0 133.8 jit_solution(3817603030935058602)
XLA Ops:
  0.6 127.9 %shard_map.112 = (bf16[32,2048]{1,0:T(8,128)(2,1)}, f32[128,1024]{1,0:T(8,128)}, f32[1024,128]{1,0:T(8,128)}) custom-call(bf16[32,2048]{1,0:T(8,128)(2,1)} %queries.1, bf16[1,512,1024]{2,1,0:T(8,128)(2,1)} %keys.1, bf16[1,512,1024]{2,1,0:T(8,128)(2,1)} %values.1, s32[1,32]{1,0:T(1,128)} %bitcast.6, s32[1,32]{1,0:T(1,128)} %bitcast.7, ...), custom_call_target="tpu_custom_call" | custom-call | tf_op jit(solution)/shard_map/pallas_call | solution.py:696
  128.5 1.6 %copy.15 = bf16[32,2048]{1,0:T(8,128)(2,1)} copy(bf16[32,2048]{1,0:T(8,128)(2,1)} %get-tuple-element.6) | data formatting | bytes 262144
  130.1 1.9 %copy.16 = f32[128,1024]{1,0:T(8,128)} copy(f32[128,1024]{1,0:T(8,128)} %get-tuple-element.7) | data formatting | bytes 1048576
  131.9 1.9 %copy.17 = f32[1024,128]{1,0:T(8,128)} copy(f32[1024,128]{1,0:T(8,128)} %get-tuple-element.8) | data formatting | bytes 1048576

commit v2 on v1

--- a/solution.py
+++ b/solution.py
@@ -27,7 +27,7 @@
 GRAD_SCALE = 2.0 / ALL_ROWS
 SPARSE_SCALE = 1.0 / ALL_ROWS
 
-N_SEMS = 264
+N_SEMS = 300
 
 
 def dot(a, b):
@@ -196,115 +196,6 @@
             )
     arrived[own16, :] = outgoing[own16, :]
     notes_in[own8, :] = notes_out[own8, :]
-    for c in waits:
-        c.wait_recv()
-    note = notes_in[0:8, :]
-    for s in range(1, N_DP):
-        note = note + notes_in[s * 8:(s + 1) * 8, :]
-    place_q = jnp.broadcast_to(note[0:1, :], (256, 256)).astype(jnp.int32)
-    put = lax.shift_right_logical(sub_q, 5) == (lane_q & 7)
-    put = put & ((sub_q & 31) == place_q)
-    placed = dot(jnp.where(put, 1.0, 0.0).astype(BF16), arrived[...]).astype(BF16)
-
-    def block(zb, cb, offset=0, size=ROWS_DEV):
-        return pl.ds(pl.multiple_of((cb * N_Z + zb) * ROWS_DEV + offset, 16), size)
-
-    def chip(k):
-        return lax.rem(z + k + N_Z, N_Z)
-
-    own = block(z, core)
-    for h in range(HEADS):
-        gathered[own, h * 256:(h + 1) * 256] = placed[h * 32:(h + 1) * 32, :]
-    tile = jnp.broadcast_to(note[1:2, 0:128], (8, 128))
-    energies[me_l] = tile
-
-    def gather_events(buf, pieces):
-        size = ROWS_DEV // pieces
-        half = ROWS_DEV // 2
-        plan = {}
-        for sign in (1, -1):
-            for k in range(1, 5):
-                if k < 4:
-                    parts = [(p * size, size) for p in range(pieces)]
-                else:
-                    parts = [(0 if sign == 1 else half, half)]
-                for off, sz in parts:
-                    src_z = chip(-sign * (k - 1))
-                    ref = buf.at[block(src_z, core, off, sz)]
-                    got = chip(-sign * k)
-                    copy = remote(ref, ref, at_z(sign))
-                    got_ref = buf.at[block(got, core, off, sz)]
-                    arrival = pltpu.make_async_remote_copy(
-                        src_ref=got_ref, dst_ref=got_ref, send_sem=send_sems.at[counter[0] - 1],
-                        recv_sem=recv_sems.at[counter[0] - 1], device_id=at_z(sign), device_id_type=MESH,
-                    )
-                    pass_on = remote(got_ref, got_ref, partner)
-                    other_ref = buf.at[block(got, other, off, sz)]
-                    passed = pltpu.make_async_remote_copy(
-                        src_ref=other_ref, dst_ref=other_ref, send_sem=send_sems.at[counter[0] - 1],
-                        recv_sem=recv_sems.at[counter[0] - 1], device_id=partner, device_id_type=MESH,
-                    )
-                    plan[(sign, k, off)] = (copy, arrival, pass_on, passed, sz)
-        own_ref = buf.at[own]
-        own_pass = remote(own_ref, own_ref, partner)
-        own_other = buf.at[block(z, other)]
-        own_passed = pltpu.make_async_remote_copy(
-            src_ref=own_other, dst_ref=own_other, send_sem=send_sems.at[counter[0] - 1],
-            recv_sem=recv_sems.at[counter[0] - 1], device_id=partner, device_id_type=MESH,
-        )
-
-        def first():
-            for p in range(pieces):
-                for sign in (1, -1):
-                    start(plan[(sign, 1, p * size)][0])
-            start(own_pass)
-
-        def step(k):
-            offs = [p * size for p in range(pieces)]
-            for n in range(pieces):
-                for sign in (1, -1):
-                    if k < 4:
-                        off = offs[n] if sign == 1 else offs[pieces - 1 - n]
-                        off = offs[n]
-                    else:
-                        if n > 0:
-                            continue
-                        off = 0 if sign == 1 else half
-                    copy, arrival, pass_on, passed, sz = plan[(sign, k, off)]
-                    arrival.wait_recv()
-                    if k < 3:
-                        start(plan[(sign, k + 1, off)][0])
-                    elif k == 3:
-                        wanted = 0 if sign == 1 else half
-                        if pieces == 1 or off == wanted:
-                            start(plan[(sign, 4, wanted)][0])
-                    start(pass_on)
-
-        def finish(k):
-            if k == 0:
-                own_passed.wait_recv()
-                return
-            for key, item in plan.items():
-                if key[1] == abs(k) and (abs(k) == 4 or key[0] == (1 if k > 0 else -1)):
-                    item[3].wait_recv()
-
-        return first, step, finish
-
-    first, step, finish = gather_events(gathered, 2)
-    first()
-    e_waits = []
-    for o in range(1, N_DP):
-        to = lax.rem(me_l + o, N_DP)
-        frm = lax.rem(me_l + N_DP - o, N_DP)
-        i = counter[0]
-        start(remote(energies.at[me_l], energies.at[me_l], {"latent": to}))
-        e_waits.append(
-            pltpu.make_async_remote_copy(
-                src_ref=energies.at[me_l], dst_ref=energies.at[frm], send_sem=send_sems.at[i],
-                recv_sem=recv_sems.at[i], device_id={"latent": to}, device_id_type=MESH,
-            )
-        )
-
     for c in load_d:
         c.wait()
     diag = iota((128, 128), 0) == iota((128, 128), 1)
@@ -320,6 +211,138 @@
         )
         dec_coef[b * 128:(b + 1) * 128, :] = jnp.broadcast_to(SPARSE_SCALE / norm, (128, 128))
 
+    for c in waits:
+        c.wait_recv()
+    note = notes_in[0:8, :]
+    for s in range(1, N_DP):
+        note = note + notes_in[s * 8:(s + 1) * 8, :]
+    place_q = jnp.broadcast_to(note[0:1, :], (256, 256)).astype(jnp.int32)
+    put = lax.shift_right_logical(sub_q, 5) == (lane_q & 7)
+    put = put & ((sub_q & 31) == place_q)
+    placed = dot(jnp.where(put, 1.0, 0.0).astype(BF16), arrived[...]).astype(BF16)
+
+    def block(zb, cb, offset=0, size=ROWS_DEV):
+        return pl.ds(pl.multiple_of((cb * N_Z + zb) * ROWS_DEV + offset, 16), size)
+
+    def chip(k):
+        return lax.rem(z + k + N_Z, N_Z)
+
+    own = block(z, core)
+    half = ROWS_DEV // 2
+
+    def hop(buf, zb, offset, size, device, arrives):
+        ref = buf.at[block(zb, core, offset, size)]
+        copy = remote(ref, ref, device)
+        got_ref = buf.at[block(arrives, core, offset, size)]
+        arrival = same_semaphores(got_ref, device)
+        pass_on = remote(got_ref, got_ref, partner)
+        passed = same_semaphores(buf.at[block(arrives, other, offset, size)], partner)
+        return copy, arrival, pass_on, passed
+
+    def same_semaphores(ref, device):
+        i = counter[0] - 1
+        return pltpu.make_async_remote_copy(
+            src_ref=ref, dst_ref=ref, send_sem=send_sems.at[i], recv_sem=recv_sems.at[i],
+            device_id=device, device_id_type=MESH,
+        )
+
+    def own_hop(buf):
+        pass_on = remote(buf.at[own], buf.at[own], partner)
+        return pass_on, same_semaphores(buf.at[block(z, other)], partner)
+
+    def ring_gather(buf):
+        plan = {}
+        for k in range(1, 5):
+            for sign in (1, -1):
+                off, size = (0, ROWS_DEV) if k < 4 else (0 if sign == 1 else half, half)
+                plan[(sign, k)] = hop(buf, chip(-sign * (k - 1)), off, size, at_z(sign), chip(-sign * k))
+        own_pass, own_passed = own_hop(buf)
+
+        def first():
+            start(plan[(1, 1)][0])
+            start(plan[(-1, 1)][0])
+            start(own_pass)
+
+        def step(k):
+            for sign in (1, -1):
+                plan[(sign, k)][1].wait_recv()
+                if k < 4:
+                    start(plan[(sign, k + 1)][0])
+                start(plan[(sign, k)][2])
+
+        def finish(k):
+            if k == 0:
+                own_passed.wait_recv()
+            elif abs(k) == 4:
+                plan[(1, 4)][3].wait_recv()
+                plan[(-1, 4)][3].wait_recv()
+            else:
+                plan[(1 if k < 0 else -1, abs(k))][3].wait_recv()
+
+        return first, step, finish
+
+    def quick_gather(buf):
+        near, far, third, fourth = {}, {}, {}, {}
+        for sign in (1, -1):
+            far[sign] = hop(buf, z, 0, ROWS_DEV, at_z(2 * sign), chip(-2 * sign))
+            near[sign] = hop(buf, z, 0, ROWS_DEV, at_z(sign), chip(-sign))
+            third[sign] = hop(buf, chip(-2 * sign), 0, ROWS_DEV, at_z(sign), chip(-3 * sign))
+            fourth[sign] = hop(buf, chip(-2 * sign), 0 if sign == 1 else half, half, at_z(2 * sign), chip(4))
+        own_pass, own_passed = own_hop(buf)
+
+        def first():
+            for group in (far, near):
+                for sign in (1, -1):
+                    start(group[sign][0])
+            start(own_pass)
+
+        def middle():
+            for sign in (1, -1):
+                far[sign][1].wait_recv()
+                start(fourth[sign][0])
+                start(third[sign][0])
+                start(far[sign][2])
+            for sign in (1, -1):
+                near[sign][1].wait_recv()
+                start(near[sign][2])
+
+        def last():
+            for group in (third, fourth):
+                for sign in (1, -1):
+                    group[sign][1].wait_recv()
+                    start(group[sign][2])
+
+        def finish():
+            own_passed.wait_recv()
+            for group in (far, near, third, fourth):
+                for sign in (1, -1):
+                    group[sign][3].wait_recv()
+
+        return first, middle, last, finish
+
+    for h in range(HEADS):
+        gathered[h // 2, own, (h % 2) * 256:(h % 2 + 1) * 256] = placed[h * 32:(h + 1) * 32, :]
+    energies[me_l] = jnp.broadcast_to(note[1:2, 0:128], (8, 128))
+    e_waits = []
+    for o in range(1, N_DP):
+        to = lax.rem(me_l + o, N_DP)
+        frm = lax.rem(me_l + N_DP - o, N_DP)
+        start(remote(energies.at[me_l], energies.at[me_l], {"latent": to}))
+        e_waits.append(same_semaphores(energies.at[frm], {"latent": to}))
+    rings = [ring_gather(gathered.at[c]) for c in range(CHUNKS)]
+
+    def step(k):
+        for ring in rings:
+            ring[1](k)
+
+    def finish(*ks):
+        for ring in rings:
+            for k in ks:
+                ring[2](k)
+
+    for ring in rings:
+        ring[0]()
+    step(1)
     for c in e_waits:
         c.wait_recv()
     total = energies[0]
@@ -332,9 +355,10 @@
     def encode(chips):
         spots = [block(zb, cb) for zb in chips for cb in range(2)]
         for n, spot in enumerate(spots):
-            scaled = (gathered[spot, :].astype(F32) * norm_scale).astype(BF16)
-            inputs[spot, :] = scaled
-            batch[n * ROWS_DEV:(n + 1) * ROWS_DEV, :] = scaled
+            for c in range(CHUNKS):
+                scaled = (gathered[c, spot, :].astype(F32) * norm_scale).astype(BF16)
+                inputs[spot, c * COLS:(c + 1) * COLS] = scaled
+                batch[n * ROWS_DEV:(n + 1) * ROWS_DEV, c * COLS:(c + 1) * COLS] = scaled
 
         def tile_step(t, carry):
             at = pl.ds(pl.multiple_of(t * 256, 256), 256)
@@ -351,21 +375,16 @@
 
         lax.fori_loop(0, LAT // 256, tile_step, 0)
 
-    step(1)
-    finish(0)
-    finish(1)
+    step(2)
+    finish(0, -1)
     encode((z, chip(-1)))
-    step(2)
-    finish(-1)
-    finish(2)
+    step(3)
+    finish(1, -2)
     encode((chip(1), chip(-2)))
-    step(3)
-    finish(-2)
-    finish(3)
+    finish(2, -3)
     encode((chip(2), chip(-3)))
     step(4)
-    finish(-3)
-    finish(4)
+    finish(3, 4)
     encode((chip(3), chip(4)))
 
     events = []
@@ -375,7 +394,6 @@
 
     own_half = pl.ds(pl.multiple_of(core * 256, 256), 256)
     other_half = pl.ds(pl.multiple_of(other * 256, 256), 256)
-    STEP = 2.3
 
     def transpose_coded(b):
         def run():
@@ -393,11 +411,12 @@
         return run
 
     for b in range(4):
-        at_time(5.0 + 2.4 * b, transpose_coded(b))
-        at_time(6.2 + 2.4 * b, transpose_inputs(b))
+        at_time((2.5, 2.6, 4.5, 4.6)[b], transpose_coded(b))
+        at_time((6.5, 9.0, 11.0, 13.2)[b], transpose_inputs(b))
 
     def latent_stream(j):
-        base = 1.0 * j
+        begin = (0.0, 1.0, 3.0, 7.0)[j]
+        base = (2.2, 4.2, 8.4, 12.8)[j]
         swap = remote(part_send.at[j], part_recv.at[j], partner)
 
         def start_half():
@@ -407,45 +426,47 @@
         def own_part():
             part_own[j] = dot(coded[own_half, :], dec_v[j])
 
-        ring = {}
-        for sign, out_buf, in_buf in ((1, rs_send_p, rs_recv_p), (-1, rs_send_m, rs_recv_m)):
-            for t in range(4):
-                if t == 0:
-                    rows = slice(0, 16) if sign == 1 else slice(16, 32)
-                else:
-                    rows = slice(0, 32)
-                ring[(sign, t)] = remote(out_buf.at[j, t, rows], in_buf.at[j, t, rows], at_z(sign))
+        sides = ((1, rs_send_p, rs_recv_p), (-1, rs_send_m, rs_recv_m))
+        hops = {}
+        for sign, out_buf, in_buf in sides:
+            near = slice(0, 16) if sign == 1 else slice(16, 32)
+            for slot, dist in ((0, 2), (1, 1), (2, 2), (3, 1)):
+                rows = near if slot == 0 else slice(0, 32)
+                hops[(sign, slot)] = remote(out_buf.at[j, slot, rows], in_buf.at[j, slot, rows], at_z(dist * sign))
 
         def own_block(zb):
             rows = pl.ds(pl.multiple_of(zb * ROWS_DEV, ROWS_DEV), ROWS_DEV)
             return part_own[j, rows, :] + part_recv[j, rows, :].astype(F32)
 
-        def reduce_step(t):
-            def run():
-                if t == 0:
-                    swap.wait_recv()
-                for sign, out_buf, in_buf in ((1, rs_send_p, rs_recv_p), (-1, rs_send_m, rs_recv_m)):
-                    mine_ = own_block(chip(sign * (4 - t)))
+        def reduce_first():
+            swap.wait_recv()
+            for slot, dist in ((0, 4), (1, 3), (3, 1)):
+                for sign, out_buf, in_buf in sides:
+                    mine_ = own_block(chip(sign * dist))
                     near = slice(0, 16) if sign == 1 else slice(16, 32)
-                    far = slice(16, 32) if sign == 1 else slice(0, 16)
-                    if t == 0:
-                        out_buf[j, 0, near, :] = mine_[near, :].astype(BF16)
-                    else:
-                        ring[(sign, t - 1)].wait_recv()
-                        if t == 1:
-                            out_buf[j, 1, near, :] = (mine_[near, :] + in_buf[j, 0, near, :].astype(F32)).astype(BF16)
-                            out_buf[j, 1, far, :] = mine_[far, :].astype(BF16)
-                        else:
-                            out_buf[j, t, :, :] = (mine_ + in_buf[j, t - 1, :, :].astype(F32)).astype(BF16)
-                    start(ring[(sign, t)])
-            return run
-
-        first_, step_, finish_ = gather_events(residual.at[j], 1)
+                    rows = near if slot == 0 else slice(0, 32)
+                    out_buf[j, slot, rows, :] = mine_[rows, :].astype(BF16)
+                    start(hops[(sign, slot)])
+
+        def reduce_second():
+            for sign, out_buf, in_buf in sides:
+                near = slice(0, 16) if sign == 1 else slice(16, 32)
+                far = slice(16, 32) if sign == 1 else slice(0, 16)
+                hops[(sign, 1)].wait_recv()
+                hops[(sign, 0)].wait_recv()
+                mine_ = own_block(chip(sign * 2)) + in_buf[j, 1, :, :].astype(F32)
+                out_buf[j, 2, near, :] = (mine_[near, :] + in_buf[j, 0, near, :].astype(F32)).astype(BF16)
+                out_buf[j, 2, far, :] = mine_[far, :].astype(BF16)
+                start(hops[(sign, 2)])
+
+        first_, middle_, last_, finish_ = quick_gather(residual.at[j])
 
         def own_sum():
-            ring[(1, 3)].wait_recv()
-            ring[(-1, 3)].wait_recv()
-            summed = own_block(z) + rs_recv_p[j, 3, :, :].astype(F32) + rs_recv_m[j, 3, :, :].astype(F32)
+            summed = own_block(z)
+            for slot in (3, 2):
+                for sign, out_buf, in_buf in sides:
+                    hops[(sign, slot)].wait_recv()
+                    summed = summed + in_buf[j, slot, :, :].astype(F32)
             spans = [slice(chunk_dp(j, s) * 128, chunk_dp(j, s) * 128 + 128) for s in range(N_X)]
             bias = jnp.concatenate([dec_bias[:, sp] for sp in spans], axis=1)
             rebuilt = summed + bias
@@ -456,20 +477,14 @@
             residual[j, own, :] = (rebuilt - ins).astype(BF16)
             first_()
 
-        at_time(base, start_half)
-        at_time(base + 0.5, own_part)
-        for t in range(4):
-            at_time(base + 2.5 + t * STEP, reduce_step(t))
-        at_time(base + 2.5 + 4 * STEP, own_sum)
-        for k in range(1, 5):
-            at_time(base + 2.5 + (4 + k) * STEP, lambda k=k: step_(k))
-
-        def all_in():
-            finish_(0)
-            for k in (1, -1, 2, -2, 3, -3, 4):
-                finish_(k)
-
-        return base + 2.5 + 8 * STEP + 1.0, all_in
+        at_time(begin, start_half)
+        at_time(begin + 0.5, own_part)
+        at_time(base, reduce_first)
+        at_time(base + 4.0, reduce_second)
+        at_time(base + 8.2, own_sum)
+        at_time(base + 12.6, middle_)
+        at_time(base + 16.8, last_)
+        return base + 18.2, finish_
 
     def pair_reduce(pick_ref, split, first_in, second_in, hop, me):
         a, b = (0, split), (split, split)
@@ -643,12 +658,24 @@
         copy.wait_send()
 
 
+def finish_kernel(*refs):
+    ins, outs, bufs, sems = refs[0:3], refs[3:6], refs[6:9], refs[9]
+    loads = [pltpu.make_async_copy(a, b, sems.at[0, i]) for i, (a, b) in enumerate(zip(ins, bufs))]
+    stores = [pltpu.make_async_copy(a, b, sems.at[1, i]) for i, (a, b) in enumerate(zip(bufs, outs))]
+    for c in loads:
+        c.start()
+    for a, b in zip(loads, stores):
+        a.wait()
+        b.start()
+    for c in stores:
+        c.wait()
+
+
 def shards(
     queries, cache_keys, cache_values, positions, shuffle, enc_weight, enc_bias, dec_weight, dec_bias
 ):
     any_ = pl.BlockSpec(memory_space=pl.ANY)
     vmem = pl.BlockSpec(memory_space=pltpu.VMEM)
-    quarter = ROWS_DEV // 2
     scratch = [
         ((ROWS_DEV, WIDTH), BF16),
         ((CACHE, KV_HEADS * HEAD_DIM), BF16),
@@ -661,7 +688,7 @@
         ((128, 256), F32),
         ((128, 256), F32),
         ((16, 8, 128), F32),
-        ((GROUP, WIDTH), BF16),
+        ((CHUNKS, GROUP, COLS), BF16),
         ((GROUP, WIDTH), BF16),
         ((128, WIDTH), BF16),
         ((CHUNKS, COLS, GROUP), BF16),
@@ -693,7 +720,7 @@
         ((2, 2, 32, LAT), BF16),
         ((2, 2, 64, LAT), BF16),
     ]
-    return pl.pallas_call(
+    results = pl.pallas_call(
         kernel,
         out_shape=(
             jax.ShapeDtypeStruct((ROWS_DEV, WIDTH), BF16),
@@ -715,6 +742,13 @@
         queries, cache_keys, cache_values, positions.reshape(1, -1), shuffle.reshape(1, -1),
         enc_weight, enc_bias.reshape(1, -1), dec_weight, dec_bias.reshape(1, -1),
     )
+    return pl.pallas_call(
+        finish_kernel,
+        out_shape=tuple(jax.ShapeDtypeStruct(r.shape, r.dtype) for r in results),
+        in_specs=[any_, any_, any_],
+        out_specs=(any_, any_, any_),
+        scratch_shapes=[pltpu.VMEM(r.shape, r.dtype) for r in results] + [pltpu.SemaphoreType.DMA((2, 3))],
+    )(*results)
 
 
 def solution(mesh):

time: 134 us -> 126 us (0.940)
  local copies, waits for them, and re-layouts: 5.32 us -> 0 us
  Pallas kernels: 128 us -> 124 us
    pallas_call x1, Pallas kernels: 128 us -> 122 us  [shards(): pl.pallas_call(kernel, out_shape=(jax.ShapeDtypeStruct((ROWS_DEV, WIDTH),...]
    unnamed x3 -> x0, local copies, waits for them, and re-layouts: 5.32 us -> none
    pallas_call x0 -> x1, Pallas kernels: none -> 2.13 us  [shards(): pl.pallas_call(finish_kernel, out_shape=tuple((jax.ShapeDtypeStruct(r.sha...]
where the time goes in v2:
time: 126 us; the launch traced here: 125 us
  Pallas kernels  124 us (98%)
    pallas_call x1, Pallas kernels, shards(): pl.pallas_call(kernel, out_shape=(jax.ShapeDtypeStruct((ROWS_DEV, WIDTH),...  122 us

profile of v2, /device:TPU:32, one launch (start us, length us, event | category | flops | bytes accessed | tf_op | source)
XLA Modules:
  0.0 125.0 jit_solution(10223984990905032227)
XLA Ops:
  0.6 122.1 %shard_map.112 = (bf16[32,2048]{1,0:T(8,128)(2,1)}, f32[128,1024]{1,0:T(8,128)}, f32[1024,128]{1,0:T(8,128)}) custom-call(bf16[32,2048]{1,0:T(8,128)(2,1)} %queries.1, bf16[1,512,1024]{2,1,0:T(8,128)(2,1)} %keys.1, bf16[1,512,1024]{2,1,0:T(8,128)(2,1)} %values.1, s32[1,32]{1,0:T(1,128)} %bitcast.6, s32[1,32]{1,0:T(1,128)} %bitcast.7, ...), custom_call_target="tpu_custom_call" | custom-call | tf_op jit(solution)/shard_map/pallas_call | solution.py:723
  122.7 2.1 %shard_map.113 = (bf16[32,2048]{1,0:T(8,128)(2,1)}, f32[128,1024]{1,0:T(8,128)}, f32[1024,128]{1,0:T(8,128)}) custom-call(bf16[32,2048]{1,0:T(8,128)(2,1)} %get-tuple-element.6.refs_0_, f32[128,1024]{1,0:T(8,128)} %get-tuple-element.7.refs_1_, f32[1024,128]{1,0:T(8,128)} %get-tuple-element.8.refs_2_), custom_call_target="tpu_custom_call" | custom-call | tf_op jit(solution)/shard_map/pallas_call | solution.py:745

commit v3 on v2

--- a/solution.py
+++ b/solution.py
@@ -97,15 +97,6 @@
     load_q = load(queries, q_v, 0)
     load_k = load(keys.at[0], k_v, 1)
     load_v = load(values.at[0], v_v, 2)
-    load_e = load(enc_w, enc_v, 3)
-    load_d = []
-    for j in range(CHUNKS):
-        for s in range(N_X):
-            d = chunk_dp(j, s)
-            load_d.append(
-                load(dec_w.at[:, d * 128:(d + 1) * 128], dec_v.at[j, :, s * 128:(s + 1) * 128], 4 + j * N_X + s)
-            )
-
     barrier = pltpu.get_barrier_semaphore()
     for o in range(1, N_DP):
         pl.semaphore_signal(barrier, inc=1, device_id={"dp": lax.rem(me_dp + o, N_DP)}, device_id_type=MESH)
@@ -142,6 +133,14 @@
     load_q.wait()
     load_k.wait()
     load_v.wait()
+    load_e = load(enc_w, enc_v, 3)
+    load_d = []
+    for j in range(CHUNKS):
+        for s in range(N_X):
+            d = chunk_dp(j, s)
+            load_d.append(
+                load(dec_w.at[:, d * 128:(d + 1) * 128], dec_v.at[j, :, s * 128:(s + 1) * 128], 4 + j * N_X + s)
+            )
     energy = jnp.zeros((1, 1), F32)
     for g in range(KV_HEADS):
         cols = slice(g * HEAD_DIM, (g + 1) * HEAD_DIM)
@@ -158,18 +157,17 @@
         energy = energy + jnp.sum(jnp.sum(square, axis=1, keepdims=True), axis=0, keepdims=True)
     outgoing[...] = dot(pick, heads[...]).astype(BF16)
 
-    note_sub = iota((128, 256), 0)
-    note_lane = iota((128, 256), 1)
+    note_lane = iota((128, 128), 1)
     peer_sub = lax.shift_right_logical(iota((128, ROWS_DEV), 0), 3)
     slot_n = jnp.broadcast_to(slot_row, (128, ROWS_DEV))
     place_n = jnp.broadcast_to(place_row, (128, ROWS_DEV))
     place = [
         jnp.sum(jnp.where(slot_n == 2 * peer_sub + k, place_n, 0.0), axis=1, keepdims=True) for k in range(2)
     ]
-    mine = lax.shift_right_logical(note_lane, 4) == me_dp
-    place_note = jnp.where((lax.shift_right_logical(note_lane, 3) & 1) == 0, place[0], place[1])
-    place_note = jnp.where(mine, place_note, 0.0)
-    notes_out[...] = jnp.where((note_sub & 7) == 0, place_note, jnp.broadcast_to(energy, (128, 256)))
+    mine = lax.shift_right_logical(note_lane, 3) == me_dp
+    place_note = jnp.where((note_lane & 4) == 0, place[0], place[1])
+    place_note = jnp.where((note_lane & 1) == 0, place_note, jnp.broadcast_to(energy, (128, 128)))
+    notes_out[...] = jnp.where(mine, place_note, 0.0)
 
     pl.semaphore_wait(barrier, 2 * (N_DP - 1))
     own16 = pl.ds(pl.multiple_of(me_dp * 16, 16), 16)
@@ -216,7 +214,14 @@
     note = notes_in[0:8, :]
     for s in range(1, N_DP):
         note = note + notes_in[s * 8:(s + 1) * 8, :]
-    place_q = jnp.broadcast_to(note[0:1, :], (256, 256)).astype(jnp.int32)
+    from_lane = iota((128, 256), 0)
+    to_lane = iota((128, 256), 1)
+    spread = lax.shift_right_logical(from_lane, 3) == lax.shift_right_logical(to_lane, 4)
+    spread = spread & ((from_lane & 7) == lax.shift_right_logical(to_lane & 8, 1))
+    places = jnp.where((iota((8, 128), 1) & 1) == 0, note, 0.0).astype(BF16)
+    places = dot(places, jnp.where(spread, 1.0, 0.0).astype(BF16))
+    place_q = jnp.broadcast_to(places[0:1, :].astype(jnp.int32), (256, 256))
+    column_energy = jnp.sum(jnp.where((iota((8, 128), 1) & 7) == 1, note, 0.0), axis=1, keepdims=True)
     put = lax.shift_right_logical(sub_q, 5) == (lane_q & 7)
     put = put & ((sub_q & 31) == place_q)
     placed = dot(jnp.where(put, 1.0, 0.0).astype(BF16), arrived[...]).astype(BF16)
@@ -250,51 +255,35 @@
         pass_on = remote(buf.at[own], buf.at[own], partner)
         return pass_on, same_semaphores(buf.at[block(z, other)], partner)
 
-    def ring_gather(buf):
-        plan = {}
-        for k in range(1, 5):
-            for sign in (1, -1):
-                off, size = (0, ROWS_DEV) if k < 4 else (0 if sign == 1 else half, half)
-                plan[(sign, k)] = hop(buf, chip(-sign * (k - 1)), off, size, at_z(sign), chip(-sign * k))
-        own_pass, own_passed = own_hop(buf)
-
-        def first():
-            start(plan[(1, 1)][0])
-            start(plan[(-1, 1)][0])
-            start(own_pass)
-
-        def step(k):
-            for sign in (1, -1):
-                plan[(sign, k)][1].wait_recv()
-                if k < 4:
-                    start(plan[(sign, k + 1)][0])
-                start(plan[(sign, k)][2])
-
-        def finish(k):
-            if k == 0:
-                own_passed.wait_recv()
-            elif abs(k) == 4:
-                plan[(1, 4)][3].wait_recv()
-                plan[(-1, 4)][3].wait_recv()
-            else:
-                plan[(1 if k < 0 else -1, abs(k))][3].wait_recv()
-
-        return first, step, finish
-
-    def quick_gather(buf):
+    def gather(buf, deep):
         near, far, third, fourth = {}, {}, {}, {}
         for sign in (1, -1):
-            far[sign] = hop(buf, z, 0, ROWS_DEV, at_z(2 * sign), chip(-2 * sign))
             near[sign] = hop(buf, z, 0, ROWS_DEV, at_z(sign), chip(-sign))
+            if deep:
+                far[sign] = hop(buf, chip(-sign), 0, ROWS_DEV, at_z(sign), chip(-2 * sign))
+            else:
+                far[sign] = hop(buf, z, 0, ROWS_DEV, at_z(2 * sign), chip(-2 * sign))
             third[sign] = hop(buf, chip(-2 * sign), 0, ROWS_DEV, at_z(sign), chip(-3 * sign))
             fourth[sign] = hop(buf, chip(-2 * sign), 0 if sign == 1 else half, half, at_z(2 * sign), chip(4))
         own_pass, own_passed = own_hop(buf)
+        passed = {0: [own_passed], 4: [fourth[1][3], fourth[-1][3]]}
+        for sign in (1, -1):
+            for k, group in ((1, near), (2, far), (3, third)):
+                passed[-sign * k] = [group[sign][3]]
 
         def first():
-            for group in (far, near):
+            if not deep:
                 for sign in (1, -1):
-                    start(group[sign][0])
+                    start(far[sign][0])
+            for sign in (1, -1):
+                start(near[sign][0])
             start(own_pass)
+
+        def relay():
+            for sign in (1, -1):
+                near[sign][1].wait_recv()
+                start(far[sign][0])
+                start(near[sign][2])
 
         def middle():
             for sign in (1, -1):
@@ -302,9 +291,10 @@
                 start(fourth[sign][0])
                 start(third[sign][0])
                 start(far[sign][2])
-            for sign in (1, -1):
-                near[sign][1].wait_recv()
-                start(near[sign][2])
+            if not deep:
+                for sign in (1, -1):
+                    near[sign][1].wait_recv()
+                    start(near[sign][2])
 
         def last():
             for group in (third, fourth):
@@ -312,36 +302,33 @@
                     group[sign][1].wait_recv()
                     start(group[sign][2])
 
-        def finish():
-            own_passed.wait_recv()
-            for group in (far, near, third, fourth):
-                for sign in (1, -1):
-                    group[sign][3].wait_recv()
-
-        return first, middle, last, finish
+        def finish(names=tuple(passed)):
+            for name in names:
+                for copy in passed[name]:
+                    copy.wait_recv()
+
+        return ([first, relay, middle, last] if deep else [first, middle, last]), finish
 
     for h in range(HEADS):
         gathered[h // 2, own, (h % 2) * 256:(h % 2 + 1) * 256] = placed[h * 32:(h + 1) * 32, :]
-    energies[me_l] = jnp.broadcast_to(note[1:2, 0:128], (8, 128))
+    energies[me_l] = jnp.broadcast_to(column_energy, (8, 128))
     e_waits = []
     for o in range(1, N_DP):
         to = lax.rem(me_l + o, N_DP)
         frm = lax.rem(me_l + N_DP - o, N_DP)
         start(remote(energies.at[me_l], energies.at[me_l], {"latent": to}))
         e_waits.append(same_semaphores(energies.at[frm], {"latent": to}))
-    rings = [ring_gather(gathered.at[c]) for c in range(CHUNKS)]
+    rings = [gather(gathered.at[c], True) for c in range(CHUNKS)]
 
     def step(k):
         for ring in rings:
-            ring[1](k)
-
-    def finish(*ks):
+            ring[0][k]()
+
+    def finish(*names):
         for ring in rings:
-            for k in ks:
-                ring[2](k)
-
-    for ring in rings:
-        ring[0]()
+            ring[1](names)
+
+    step(0)
     step(1)
     for c in e_waits:
         c.wait_recv()
@@ -362,7 +349,7 @@
 
         def tile_step(t, carry):
             at = pl.ds(pl.multiple_of(t * 256, 256), 256)
-            pre = 4.0 * (dot(batch[...], enc_v[:, at]) + enc_bias[:, at])
+            pre = 4.0 * (dot(batch[0:len(spots) * ROWS_DEV, :], enc_v[:, at]) + enc_bias[:, at])
             small = jnp.exp(-jnp.abs(pre))
             active = 0.25 * (jnp.maximum(pre, 0.0) + jnp.log1p(small))
             sig = jnp.where(pre >= 0, 1.0, small) / (1.0 + small)
@@ -378,14 +365,11 @@
     step(2)
     finish(0, -1)
     encode((z, chip(-1)))
+    finish(1, 2)
+    encode((chip(1), chip(2)))
     step(3)
-    finish(1, -2)
-    encode((chip(1), chip(-2)))
-    finish(2, -3)
-    encode((chip(2), chip(-3)))
-    step(4)
-    finish(3, 4)
-    encode((chip(3), chip(4)))
+    finish(-2, 3, -3, 4)
+    encode((chip(-2), chip(3), chip(-3), chip(4)))
 
     events = []
 
@@ -411,12 +395,18 @@
         return run
 
     for b in range(4):
-        at_time((2.5, 2.6, 4.5, 4.6)[b], transpose_coded(b))
-        at_time((6.5, 9.0, 11.0, 13.2)[b], transpose_inputs(b))
+        at_time((2.5, 6.6, 6.7, 9.1)[b], transpose_coded(b))
+        at_time((11.1, 13.3, 15.6, 17.1)[b], transpose_inputs(b))
 
     def latent_stream(j):
-        begin = (0.0, 1.0, 3.0, 7.0)[j]
-        base = (2.2, 4.2, 8.4, 12.8)[j]
+        deep = j >= 2
+        begin = (0.0, 1.0, 3.8, 4.8)[j]
+        times = (
+            (2.2, 6.0, 10.2, 14.4, 18.2, 19.4),
+            (3.6, 8.5, 13.0, 18.0, 22.5, 24.0),
+            (5.0, 9.0, 13.2, 17.0, 20.5, 24.2, 27.5, 29.0),
+            (6.5, 11.0, 15.5, 20.0, 23.5, 27.6, 31.5, 33.0),
+        )[j]
         swap = remote(part_send.at[j], part_recv.at[j], partner)
 
         def start_half():
@@ -430,7 +420,7 @@
         hops = {}
         for sign, out_buf, in_buf in sides:
             near = slice(0, 16) if sign == 1 else slice(16, 32)
-            for slot, dist in ((0, 2), (1, 1), (2, 2), (3, 1)):
+            for slot, dist in ((0, 2), (1, 1), (2, 1 if deep else 2), (3, 1)):
                 rows = near if slot == 0 else slice(0, 32)
                 hops[(sign, slot)] = remote(out_buf.at[j, slot, rows], in_buf.at[j, slot, rows], at_z(dist * sign))
 
@@ -440,7 +430,7 @@
 
         def reduce_first():
             swap.wait_recv()
-            for slot, dist in ((0, 4), (1, 3), (3, 1)):
+            for slot, dist in ((0, 4), (1, 3)) if deep else ((0, 4), (1, 3), (3, 1)):
                 for sign, out_buf, in_buf in sides:
                     mine_ = own_block(chip(sign * dist))
                     near = slice(0, 16) if sign == 1 else slice(16, 32)
@@ -459,11 +449,17 @@
                 out_buf[j, 2, far, :] = mine_[far, :].astype(BF16)
                 start(hops[(sign, 2)])
 
-        first_, middle_, last_, finish_ = quick_gather(residual.at[j])
+        def reduce_third():
+            for sign, out_buf, in_buf in sides:
+                hops[(sign, 2)].wait_recv()
+                out_buf[j, 3, :, :] = (own_block(chip(sign)) + in_buf[j, 2, :, :].astype(F32)).astype(BF16)
+                start(hops[(sign, 3)])
+
+        spread_steps, finish_ = gather(residual.at[j], deep)
 
         def own_sum():
             summed = own_block(z)
-            for slot in (3, 2):
+            for slot in (3,) if deep else (3, 2):
                 for sign, out_buf, in_buf in sides:
                     hops[(sign, slot)].wait_recv()
                     summed = summed + in_buf[j, slot, :, :].astype(F32)
@@ -475,16 +471,14 @@
                 rebuilt_out[:, sp] = rebuilt_half[:, s * 128:(s + 1) * 128]
             ins = jnp.concatenate([inputs[own, sp] for sp in spans], axis=1).astype(F32)
             residual[j, own, :] = (rebuilt - ins).astype(BF16)
-            first_()
-
+            spread_steps[0]()
+
+        steps = [reduce_first, reduce_second] + ([reduce_third] if deep else []) + [own_sum] + spread_steps[1:]
         at_time(begin, start_half)
         at_time(begin + 0.5, own_part)
-        at_time(base, reduce_first)
-        at_time(base + 4.0, reduce_second)
-        at_time(base + 8.2, own_sum)
-        at_time(base + 12.6, middle_)
-        at_time(base + 16.8, last_)
-        return base + 18.2, finish_
+        for step_at, fn in zip(times, steps):
+            at_time(step_at, fn)
+        return times[-1], finish_
 
     def pair_reduce(pick_ref, split, first_in, second_in, hop, me):
         a, b = (0, split), (split, split)
@@ -631,7 +625,7 @@
     ready = 0.0
     for j in range(CHUNKS):
         t, all_in = latent_stream(j)
-        ready = max(t, ready + 2.0)
+        ready = t
         at_time(ready, all_in)
         at_time(ready + 0.1, dec_grad(j))
         at_time(ready + 0.2, act_grad(j))
@@ -685,12 +679,12 @@
         ((256, 256), BF16),
         ((256, 256), BF16),
         ((256, 256), BF16),
-        ((128, 256), F32),
-        ((128, 256), F32),
+        ((128, 128), F32),
+        ((128, 128), F32),
         ((16, 8, 128), F32),
         ((CHUNKS, GROUP, COLS), BF16),
         ((GROUP, WIDTH), BF16),
-        ((128, WIDTH), BF16),
+        ((256, WIDTH), BF16),
         ((CHUNKS, COLS, GROUP), BF16),
         ((GROUP, LAT), BF16),
         ((LAT, GROUP), BF16),

time: 126 us -> 127 us (level)
  Pallas kernels: 124 us -> 126 us
    pallas_call x1, Pallas kernels: 122 us -> 124 us  [shards(): pl.pallas_call(kernel, out_shape=(jax.ShapeDtypeStruct((ROWS_DEV, WIDTH),...]
where the time goes in v3:
time: 127 us
  Pallas kernels  126 us (99%)
    pallas_call x1, Pallas kernels, shards(): pl.pallas_call(kernel, out_shape=(jax.ShapeDtypeStruct((ROWS_DEV, WIDTH),...  124 us

profile of v3, /device:TPU:32, one launch (start us, length us, event | category | flops | bytes accessed | tf_op | source)
XLA Modules:
  0.0 127.1 jit_solution(4908986610625945820)
XLA Ops:
  0.6 124.2 %shard_map.112 = (bf16[32,2048]{1,0:T(8,128)(2,1)}, f32[128,1024]{1,0:T(8,128)}, f32[1024,128]{1,0:T(8,128)}) custom-call(bf16[32,2048]{1,0:T(8,128)(2,1)} %queries.1, bf16[1,512,1024]{2,1,0:T(8,128)(2,1)} %keys.1, bf16[1,512,1024]{2,1,0:T(8,128)(2,1)} %values.1, s32[1,32]{1,0:T(1,128)} %bitcast.6, s32[1,32]{1,0:T(1,128)} %bitcast.7, ...), custom_call_target="tpu_custom_call" | custom-call | tf_op jit(solution)/shard_map/pallas_call | solution.py:717
  124.8 2.1 %shard_map.113 = (bf16[32,2048]{1,0:T(8,128)(2,1)}, f32[128,1024]{1,0:T(8,128)}, f32[1024,128]{1,0:T(8,128)}) custom-call(bf16[32,2048]{1,0:T(8,128)(2,1)} %get-tuple-element.6.refs_0_, f32[128,1024]{1,0:T(8,128)} %get-tuple-element.7.refs_1_, f32[1024,128]{1,0:T(8,128)} %get-tuple-element.8.refs_2_), custom_call_target="tpu_custom_call" | custom-call | tf_op jit(solution)/shard_map/pallas_call | solution.py:739

commit v4 on v3

--- a/solution.py
+++ b/solution.py
@@ -53,7 +53,7 @@
     energies, gathered, inputs, batch, inputs_t, coded, coded_t, gate, norm_row, dec_coef,
     part_send, part_recv, part_own, rs_send_p, rs_recv_p, rs_send_m, rs_recv_m,
     residual, grad_act, grad_pre, dec_term, enc_term,
-    dec_r1, dec_r2, enc_r1, enc_r2, dec_u, enc_u, dec_s1, dec_s2, enc_s1, enc_s2,
+    dec_r1, dec_r2, enc_r1, enc_r2, dec_u, enc_u, dec_s1, dec_s2, enc_s,
     send_sems, recv_sems, local_sems,
 ):
     me_dp = lax.axis_index("dp")
@@ -399,13 +399,13 @@
         at_time((11.1, 13.3, 15.6, 17.1)[b], transpose_inputs(b))
 
     def latent_stream(j):
-        deep = j >= 2
-        begin = (0.0, 1.0, 3.8, 4.8)[j]
+        deep = j >= 9
+        begin = (0.0, 1.0, 3.0, 7.0)[j]
         times = (
             (2.2, 6.0, 10.2, 14.4, 18.2, 19.4),
             (3.6, 8.5, 13.0, 18.0, 22.5, 24.0),
-            (5.0, 9.0, 13.2, 17.0, 20.5, 24.2, 27.5, 29.0),
-            (6.5, 11.0, 15.5, 20.0, 23.5, 27.6, 31.5, 33.0),
+            (8.4, 12.4, 16.6, 21.0, 25.2, 26.6),
+            (12.8, 16.8, 21.0, 25.4, 29.6, 31.0),
         )[j]
         swap = remote(part_send.at[j], part_recv.at[j], partner)
 
@@ -512,7 +512,26 @@
 
         return go, combine, total
 
-    def grad_stream(term, halves, r1, r2, u, s1, s2, out, rows):
+    def direct_reduce(pick_ref, rows, arrivals, hop, me):
+        copies = [
+            remote(pick_ref(lax.rem(me + k, N_X), (0, rows)), arrivals.at[i], hop(k))
+            for i, k in enumerate((2, 1, 3))
+        ]
+
+        def go():
+            for copy in copies:
+                start(copy)
+
+        def total():
+            out = pick_ref(me, (0, rows))[...].astype(F32)
+            for i in (1, 2, 0):
+                copies[i].wait_recv()
+                out = out + arrivals[i].astype(F32)
+            return out
+
+        return go, None, total
+
+    def grad_stream(term, r1, r2, u, s1, s2, out, rows):
         half = rows // 2
         split = half // 2
         parts = []
@@ -537,7 +556,10 @@
                 j = lax.rem(i + (x if o == 0 else y), N_X)
                 return u.at[o, j, pl.ds(part[0], part[1])]
 
-            tail.append(pair_reduce(pick_ref, split, s1.at[o], s2.at[o], hop, me))
+            if s1 is None:
+                tail.append(direct_reduce(pick_ref, half, s2.at[o], hop, me))
+            else:
+                tail.append(pair_reduce(pick_ref, split, s1.at[o], s2.at[o], hop, me))
 
         def fold(j):
             def run():
@@ -570,10 +592,10 @@
         return go, combine, fold, tail_go, tail_combine, tail_total
 
     dec_go, dec_combine, dec_fold, dec_tail_go, dec_tail_combine, dec_tail_total = grad_stream(
-        dec_term, None, dec_r1, dec_r2, dec_u, dec_s1, dec_s2, dec_out, LAT
+        dec_term, dec_r1, dec_r2, dec_u, dec_s1, dec_s2, dec_out, LAT
     )
-    enc_go, enc_combine, enc_fold, enc_tail_go, enc_tail_combine, enc_tail_total = grad_stream(
-        enc_term, None, enc_r1, enc_r2, enc_u, enc_s1, enc_s2, enc_out, 128
+    enc_go, enc_combine, enc_fold, enc_tail_go, _, enc_tail_total = grad_stream(
+        enc_term, enc_r1, enc_r2, enc_u, None, enc_s, enc_out, 128
     )
 
     def dec_grad(j):
@@ -643,26 +665,12 @@
     at_time(dec_end + 5.0, dec_tail_combine)
     at_time(dec_end + 12.0, dec_tail_total)
     at_time(enc_end + 0.1, enc_tail_go)
-    at_time(enc_end + 3.5, enc_tail_combine)
     at_time(enc_end + 8.0, enc_tail_total)
 
     for _, _, fn in sorted(events, key=lambda e: (e[0], e[1])):
         fn()
     for copy in sent:
         copy.wait_send()
-
-
-def finish_kernel(*refs):
-    ins, outs, bufs, sems = refs[0:3], refs[3:6], refs[6:9], refs[9]
-    loads = [pltpu.make_async_copy(a, b, sems.at[0, i]) for i, (a, b) in enumerate(zip(ins, bufs))]
-    stores = [pltpu.make_async_copy(a, b, sems.at[1, i]) for i, (a, b) in enumerate(zip(bufs, outs))]
-    for c in loads:
-        c.start()
-    for a, b in zip(loads, stores):
-        a.wait()
-        b.start()
-    for c in stores:
-        c.wait()
 
 
 def shards(
@@ -711,15 +719,14 @@
         ((2, CHUNKS, 64, LAT), BF16),
         ((2, 2, 256, 128), BF16),
         ((2, 2, 512, 128), BF16),
-        ((2, 2, 32, LAT), BF16),
-        ((2, 2, 64, LAT), BF16),
+        ((2, 3, 64, LAT), BF16),
     ]
-    results = pl.pallas_call(
+    return pl.pallas_call(
         kernel,
         out_shape=(
-            jax.ShapeDtypeStruct((ROWS_DEV, WIDTH), BF16),
-            jax.ShapeDtypeStruct((128, LAT), F32),
-            jax.ShapeDtypeStruct((LAT, 128), F32),
+            pltpu.VMEM((ROWS_DEV, WIDTH), BF16),
+            pltpu.VMEM((128, LAT), F32),
+            pltpu.VMEM((LAT, 128), F32),
         ),
         in_specs=[any_, any_, any_, vmem, vmem, any_, vmem, any_, vmem],
         out_specs=(vmem, vmem, vmem),
@@ -730,19 +737,12 @@
             pltpu.SemaphoreType.DMA((20,)),
         ],
         compiler_params=pltpu.CompilerParams(
-            collective_id=0, has_side_effects=True, vmem_limit_bytes=67043328
+            collective_id=0, has_side_effects=True, vmem_limit_bytes=64000000
         ),
     )(
         queries, cache_keys, cache_values, positions.reshape(1, -1), shuffle.reshape(1, -1),
         enc_weight, enc_bias.reshape(1, -1), dec_weight, dec_bias.reshape(1, -1),
     )
-    return pl.pallas_call(
-        finish_kernel,
-        out_shape=tuple(jax.ShapeDtypeStruct(r.shape, r.dtype) for r in results),
-        in_specs=[any_, any_, any_],
-        out_specs=(any_, any_, any_),
-        scratch_shapes=[pltpu.VMEM(r.shape, r.dtype) for r in results] + [pltpu.SemaphoreType.DMA((2, 3))],
-    )(*results)
 
 
 def solution(mesh):

time: 127 us -> 122 us (0.961); the launches traced: 127 us -> 120 us
  Pallas kernels: 126 us -> 117 us
  local copies, waits for them, and re-layouts: 0 us -> 2.24 us
    pallas_call x2 -> x1, Pallas kernels: 126 us -> 117 us  [shards(): pl.pallas_call(kernel, out_shape=(pltpu.VMEM((ROWS_DEV, WIDTH), BF16), pl...]
    unnamed x0 -> x3, local copies, waits for them, and re-layouts: none -> 2.24 us
where the time goes in v4:
time: 122 us; the launch traced here: 120 us
  Pallas kernels  117 us (96%)
  local copies, waits for them, and re-layouts  2.24 us (2%)
    pallas_call x1, Pallas kernels, shards(): pl.pallas_call(kernel, out_shape=(pltpu.VMEM((ROWS_DEV, WIDTH), BF16), pl...  117 us

profile of v4, /device:TPU:32, one launch (start us, length us, event | category | flops | bytes accessed | tf_op | source)
XLA Modules:
  0.0 119.8 jit_solution(9146759793759078830)
XLA Ops:
  0.6 116.9 %shard_map.112 = (bf16[32,2048]{1,0:T(8,128)(2,1)S(1)}, f32[128,1024]{1,0:T(8,128)S(1)}, f32[1024,128]{1,0:T(8,128)S(1)}) custom-call(bf16[32,2048]{1,0:T(8,128)(2,1)} %queries.1, bf16[1,512,1024]{2,1,0:T(8,128)(2,1)} %keys.1, bf16[1,512,1024]{2,1,0:T(8,128)(2,1)} %values.1, s32[1,32]{1,0:T(1,128)} %bitcast.6, s32[1,32]{1,0:T(1,128)} %bitcast.7, ...), custom_call_target="tpu_custom_call" | custom-call | tf_op jit(solution)/shard_map/pallas_call | solution.py:724
  117.6 0.7 copy.15
  118.2 0.8 copy.16
  119.0 0.8 copy.17
